TPU v7x, 512 devices: a whole 4x8x8 slice. The times are simulated.
512 devices in a mesh: ty: 16 (over x_hi, y), tx: 32 (over x_lo, z, core).
Axes of the slice: x: 4 (x_hi: 2, x_lo: 2; x = x_hi * 2 + x_lo), y: 8, z: 8, core: 2. Of those that a mesh axis runs over, the one named last changes fastest.
Arguments:
- ensemble: bfloat16 [32, 8, 128, 4096], P('tx', None, 'ty'), may hold values from -6 to 6
- diffusivity: float32 [128, 4096], P('ty', 'tx'), may hold values from 0.1 to 0.245
- vertical: float32 [8, 8], replicated, as said below
- weights: float32 [32], replicated, may hold values from 0.015625 to 0.0625
- obs_value: float32 [512, 32, 8], P(('ty', 'tx')), may hold values from -6 to 6
- obs_cell: int32 [512, 32, 8], P(('ty', 'tx')), may hold values from 0 to 8191
- obs_count: int32 [512, 32], P(('ty', 'tx')), may hold values from 0 to 8, as said below
Outputs:
- increment: float32 [8, 128, 4096], P(None, 'ty', 'tx')
- projected: float32 [512, 32, 8], P(('ty', 'tx'))
Inputs may be any that keep to these rules, and one draw needn't show every extreme that they name: `obs_count`: in every tile row one destination column, drawn from the seed, receives 8 live slots from every source of that row; other loads are uneven across destination columns. `vertical`: Banded: entries more than two levels off the diagonal are zero.
All inputs are finite; a program needn't handle non-finite values.
Results may differ from a plain program's by a relative error of at most 0.0003.
Values may be sent and summed in bfloat16 or wider, within the bound.
A program may use at most 64 MiB of HBM per device.

v0:
```python
import jax
import jax.numpy as jnp
from jax import lax
from jax.sharding import PartitionSpec as P

STEPS = 4


def padded_2(block, sides, width):
    for axis, dim in sides:
        count = lax.axis_size(axis)
        forward = [(i, i + 1) for i in range(count - 1)]
        backward = [(target, source) for source, target in forward]
        low = lax.ppermute(
            lax.slice_in_dim(block, block.shape[dim] - width, None, axis=dim), axis, forward
        )
        high = lax.ppermute(lax.slice_in_dim(block, 0, width, axis=dim), axis, backward)
        block = jnp.concatenate([low, block, high], axis=dim)
    return block


def tile_step(current, diffusivity):
    padded = padded_2(current, (("ty", 2), ("tx", 3)), 1)
    beside = (
        padded[:, :, :-2, 1:-1]
        + padded[:, :, 2:, 1:-1]
        + padded[:, :, 1:-1, :-2]
        + padded[:, :, 1:-1, 2:]
    )
    return current + diffusivity * (beside - 4.0 * current)


def shards(ensemble, diffusivity, vertical, weights, obs_value, obs_cell, obs_count):
    levels_num = ensemble.shape[1]
    tile_rows = diffusivity.shape[0]
    tile_cols = diffusivity.shape[1]
    slot_num = obs_value.shape[2]
    got_values, got_cells, got_counts = (
        lax.all_to_all(obs_value, "tx", split_axis=1, concat_axis=0, tiled=True),
        lax.all_to_all(obs_cell, "tx", split_axis=1, concat_axis=0, tiled=True),
        lax.all_to_all(obs_count, "tx", split_axis=1, concat_axis=0, tiled=True),
    )
    got_values = got_values[:, 0]
    got_cells = got_cells[:, 0]
    got_counts = got_counts[:, 0]
    live_slots = jnp.arange(slot_num, dtype=jnp.int32)[None, :] < got_counts[:, None]
    flat_cells = got_cells.ravel()
    forcing = jnp.zeros((levels_num * tile_rows * tile_cols,), jnp.float32)
    forcing = forcing.at[flat_cells].add(
        jnp.where(live_slots, got_values, jnp.float32(0.0)).ravel()
    )
    forcing = forcing.reshape(levels_num, tile_rows, tile_cols)
    tiles = lax.all_to_all(ensemble, "tx", split_axis=3, concat_axis=0, tiled=True)
    current = tiles.astype(jnp.float32) * forcing
    for repeat in range(STEPS):
        current = tile_step(current, diffusivity)
    current = jnp.einsum("lm,kmrc->klrc", vertical, current, precision=lax.Precision.HIGHEST)
    increment = jnp.einsum(
        "k,klrc->lrc", weights, tiles.astype(jnp.float32) * current, precision=lax.Precision.HIGHEST
    )
    read_back = jnp.where(
        live_slots, increment.ravel()[flat_cells].reshape(live_slots.shape), jnp.float32(0.0)
    )
    returned = lax.all_to_all(read_back[:, None, :], "tx", split_axis=0, concat_axis=1, tiled=True)
    return (increment, returned)


def solution(mesh):
    placed = (
        P("tx", None, "ty", None),
        P("ty", "tx"),
        P(),
        P(),
        P(("ty", "tx"), None, None),
        P(("ty", "tx"), None, None),
        P(("ty", "tx"), None),
    )
    return jax.shard_map(
        shards,
        mesh=mesh,
        in_specs=placed,
        out_specs=(P(None, "ty", "tx"), P(("ty", "tx"), None, None)),
        check_vma=False,
    )
```

profile of v0, /device:TPU:5, one launch (start us, length us, event | category | flops | bytes accessed | tf_op | source)
XLA Modules:
  0.0 247.4 jit_solution(8360162181086037329)
XLA Ops:
  2.0 11.8 %all-to-all-start.2 = ((s32[1,32,1]{2,0,1:T(1,128)}), s32[1,32,1]{2,0,1:T(1,128)S(1)}, u32[]{:S(2)}, u32[]{:S(2)}) async-start(s32[1,32,1]{2,0,1:T(1,128)} %copy.63), calls=%async_computation.2 | async-start | bytes 32768 | tf_op jit(solution)/shard_map/all_to_all | solution.py:41
  15.1 6.5 %all-to-all-done.2 = s32[1,32,1]{2,0,1:T(1,128)S(1)} async-done(((s32[1,32,1]{2,0,1:T(1,128)}), s32[1,32,1]{2,0,1:T(1,128)S(1)}, u32[]{:S(2)}, u32[]{:S(2)}) %all-to-all-start.2) | async-done | bytes 160 | tf_op jit(solution)/shard_map/all_to_all | solution.py:41
  21.6 4.3 %all-to-all-start.1 = ((s32[1,32,8]{2,0,1:T(1,128)}), s32[1,32,8]{2,0,1:T(1,128)S(1)}, u32[]{:S(2)}, u32[]{:S(2)}) async-start(s32[1,32,8]{2,0,1:T(1,128)} %copy.62), calls=%async_computation.1 | async-start | bytes 32768 | tf_op jit(solution)/shard_map/all_to_all | solution.py:40
  27.3 6.5 %all-to-all-done.1 = s32[1,32,8]{2,0,1:T(1,128)S(1)} async-done(((s32[1,32,8]{2,0,1:T(1,128)}), s32[1,32,8]{2,0,1:T(1,128)S(1)}, u32[]{:S(2)}, u32[]{:S(2)}) %all-to-all-start.1) | async-done | bytes 1056 | tf_op jit(solution)/shard_map/all_to_all | solution.py:40
  33.8 4.3 %all-to-all-start.3 = ((f32[1,32,8]{2,0,1:T(1,128)}), f32[1,32,8]{2,0,1:T(1,128)S(1)}, u32[]{:S(2)}, u32[]{:S(2)}) async-start(f32[1,32,8]{2,0,1:T(1,128)} %copy.64), calls=%async_computation.3 | async-start | bytes 32768 | tf_op jit(solution)/shard_map/all_to_all | solution.py:39
  38.0 8.0 %copy.59 = bf16[1,8,8,4096]{2,1,0,3:T(8,128)(2,1)} copy(bf16[1,8,8,4096]{3,2,1,0:T(8,128)(2,1)} %param.7) | data formatting | bytes 1048576 | tf_op args[0]
  46.0 11.2 %reshape.158 = bf16[32,2,4096]{2,1,0:T(2,128)(2,1)} reshape(bf16[4096,1,8,8]{3,2,1,0:T(8,128)(2,1)} %bitcast.44) | data formatting | bytes 1048576
  57.2 8.4 %all-to-all-start = ((bf16[32,2,4096]{2,1,0:T(2,128)(2,1)}), bf16[32,2,4096]{2,1,0:T(2,128)(2,1)S(1)}, u32[]{:S(2)}, u32[]{:S(2)}) async-start(bf16[32,2,4096]{2,1,0:T(2,128)(2,1)} %reshape.158), calls=%async_computation | async-start | bytes 1048576 | tf_op jit(solution)/shard_map/all_to_all | solution.py:53
  71.1 11.1 %all-to-all-done = bf16[32,2,4096]{2,1,0:T(2,128)(2,1)S(1)} async-done(((bf16[32,2,4096]{2,1,0:T(2,128)(2,1)}), bf16[32,2,4096]{2,1,0:T(2,128)(2,1)S(1)}, u32[]{:S(2)}, u32[]{:S(2)}) %all-to-all-start) | async-done | bytes 524320 | tf_op jit(solution)/shard_map/all_to_all | solution.py:53
  82.2 11.0 %reshape.159 = bf16[4096,1,8,8]{3,2,1,0:T(8,128)(2,1)} reshape(bf16[32,2,4096]{2,1,0:T(2,128)(2,1)S(1)} %all-to-all-done) | data formatting | bytes 1048576
  93.2 7.9 %copy.60 = bf16[1,8,8,4096]{3,2,1,0:T(8,128)(2,1)S(1)} copy(bf16[1,8,8,4096]{2,1,0,3:T(8,128)(2,1)} %bitcast.43) | data formatting | bytes 1048576 | tf_op jit(solution)/shard_map/all_to_all | solution.py:53
  102.3 5.3 %collective-permute-start.1 = (f32[32,8,1,128]{3,1,2,0:T(8,128)S(1)}, f32[32,8,1,128]{3,1,2,0:T(8,128)S(1)}, u32[]{:S(2)}, u32[]{:S(2)}) collective-permute-start(f32[32,8,1,128]{3,1,2,0:T(8,128)S(1)} %get-tuple-element.25), channel_id=1, source_target_pairs={{32,0},{64,32},{96,64},{128,96},{160,128},{192,160},{224,192},{256... | collective-permute-start | bytes 393224 | tf_op jit(solution)/shard_map/ppermute | solution.py:17
  109.6 7.4 %collective-permute-done = f32[32,8,1,128]{3,1,2,0:T(8,128)S(1)} collective-permute-done((f32[32,8,1,128]{3,1,2,0:T(8,128)S(1)}, f32[32,8,1,128]{3,1,2,0:T(8,128)S(1)}, u32[]{:S(2)}, u32[]{:S(2)}) %collective-permute-start) | collective-permute-done | bytes 131104 | tf_op jit(solution)/shard_map/ppermute | solution.py:14
  121.1 5.4 %collective-permute-start.3 = (f32[32,8,10,1]{0,1,3,2:T(8,128)S(1)}, f32[32,8,10,1]{0,1,3,2:T(8,128)}, u32[]{:S(2)}, u32[]{:S(2)}) collective-permute-start(f32[32,8,10,1]{0,1,3,2:T(8,128)S(1)} %copy.68), channel_id=1, source_target_pairs={{1,0},{2,1},{3,2},{4,3},{5,4},{6,5},{7,6},{8,7},{9,8},{10,9},{11,1... | collective-permute-start | bytes 30728 | tf_op jit(solution)/shard_map/ppermute | solution.py:17
  137.8 3.5 %collective-permute-start.4 = (f32[32,8,1,128]{3,1,2,0:T(8,128)S(1)}, f32[32,8,1,128]{3,1,2,0:T(8,128)S(1)}, u32[]{:S(2)}, u32[]{:S(2)}) collective-permute-start(f32[32,8,1,128]{3,1,2,0:T(8,128)S(1)} %get-tuple-element.22), channel_id=1, source_target_pairs={{0,32},{32,64},{64,96},{96,128},{128,160},{160,192},{192,224},{224... | collective-permute-start | bytes 393224 | tf_op jit(solution)/shard_map/ppermute | solution.py:14
  143.0 5.5 %collective-permute-done.4 = f32[32,8,1,128]{3,1,2,0:T(8,128)S(1)} collective-permute-done((f32[32,8,1,128]{3,1,2,0:T(8,128)S(1)}, f32[32,8,1,128]{3,1,2,0:T(8,128)S(1)}, u32[]{:S(2)}, u32[]{:S(2)}) %collective-permute-start.4) | collective-permute-done | bytes 131104 | tf_op jit(solution)/shard_map/ppermute | solution.py:14
  166.2 3.4 %collective-permute-start.8 = (f32[32,8,1,128]{3,1,2,0:T(8,128)S(1)}, f32[32,8,1,128]{3,1,2,0:T(8,128)S(1)}, u32[]{:S(2)}, u32[]{:S(2)}) collective-permute-start(f32[32,8,1,128]{3,1,2,0:T(8,128)S(1)} %get-tuple-element.20), channel_id=1, source_target_pairs={{0,32},{32,64},{64,96},{96,128},{128,160},{160,192},{192,224},{224... | collective-permute-start | bytes 393224 | tf_op jit(solution)/shard_map/ppermute | solution.py:14
  171.1 5.5 %collective-permute-done.8 = f32[32,8,1,128]{3,1,2,0:T(8,128)S(1)} collective-permute-done((f32[32,8,1,128]{3,1,2,0:T(8,128)S(1)}, f32[32,8,1,128]{3,1,2,0:T(8,128)S(1)}, u32[]{:S(2)}, u32[]{:S(2)}) %collective-permute-start.8) | collective-permute-done | bytes 131104 | tf_op jit(solution)/shard_map/ppermute | solution.py:14
  183.1 3.3 %collective-permute-start.10 = (f32[32,8,10,1]{0,1,3,2:T(8,128)S(1)}, f32[32,8,10,1]{0,1,3,2:T(8,128)S(1)}, u32[]{:S(2)}, u32[]{:S(2)}) collective-permute-start(f32[32,8,10,1]{0,1,3,2:T(8,128)S(1)} %copy.74), channel_id=1, source_target_pairs={{0,1},{1,2},{2,3},{3,4},{4,5},{5,6},{6,7},{7,8},{8,9},{9,10},{10,1... | collective-permute-start | bytes 30728 | tf_op jit(solution)/shard_map/ppermute | solution.py:14
  194.1 3.4 %collective-permute-start.12 = (f32[32,8,1,128]{3,1,2,0:T(8,128)S(1)}, f32[32,8,1,128]{3,1,2,0:T(8,128)S(1)}, u32[]{:S(2)}, u32[]{:S(2)}) collective-permute-start(f32[32,8,1,128]{3,1,2,0:T(8,128)S(1)} %get-tuple-element.18), channel_id=1, source_target_pairs={{0,32},{32,64},{64,96},{96,128},{128,160},{160,192},{192,224},{224... | collective-permute-start | bytes 393224 | tf_op jit(solution)/shard_map/ppermute | solution.py:14
  198.9 5.5 %collective-permute-done.12 = f32[32,8,1,128]{3,1,2,0:T(8,128)S(1)} collective-permute-done((f32[32,8,1,128]{3,1,2,0:T(8,128)S(1)}, f32[32,8,1,128]{3,1,2,0:T(8,128)S(1)}, u32[]{:S(2)}, u32[]{:S(2)}) %collective-permute-start.12) | collective-permute-done | bytes 131104 | tf_op jit(solution)/shard_map/ppermute | solution.py:14
  212.1 3.6 %collective-permute-start.14 = (f32[32,8,10,1]{0,1,3,2:T(8,128)}, f32[32,8,10,1]{0,1,3,2:T(8,128)}, u32[]{:S(2)}, u32[]{:S(2)}) collective-permute-start(f32[32,8,10,1]{0,1,3,2:T(8,128)} %copy.78), channel_id=1, source_target_pairs={{0,1},{1,2},{2,3},{3,4},{4,5},{5,6},{6,7},{7,8},{8,9},{9,10},{10,1... | collective-permute-start | bytes 30728 | tf_op jit(solution)/shard_map/ppermute | solution.py:14
  219.7 3.7 %fusion = f32[32,8,8,128]{3,1,2,0:T(8,128)S(1)} fusion(f32[32,8,8,128]{3,1,2,0:T(8,128)S(1)} %fusion.17, f32[32,8,10,1]{3,1,2,0:T(8,128)S(1)} %copy.81, f32[32,8,1,128]{3,1,2,0:T(8,128)S(1)} %collective-permute-done.13, f32[32,8,1,128]{3,1,2,0:T(8,128)} %copy-done.5, f32[32,8,10,1]{3,1,2,0:T(8,128)} %copy.79, f32[1,8,8,32,128]{4,3,0,2,1:T(8,128)S(1)} %bitcast.46, ...), kind=kOutput, calls=%fused_computation.3 | convolution fusion | flops 29360128 | bytes 3432704 | tf_op jit(solution)/shard_map/lm,kmrc->klrc/dot_general | solution.py:57
  226.6 20.1 %all_to_all.52 = f32[32,1,8]{2,1,0:T(1,128)S(1)} all-to-all(f32[32,1,8]{2,1,0:T(1,128)S(1)} %bitcast.49), channel_id=1, replica_groups=mesh['ty'=16,'tx'=32] {'tx'}, dimensions={0} | all-to-all | bytes 2048 | tf_op jit(solution)/shard_map/all_to_all | solution.py:64
  (98 shorter events, 79.7 us)
Async XLA Ops:
  0.6 219.1 %copy-start = (f32[8,8]{1,0:T(8,128)S(1)}, f32[8,8]{1,0:T(8,128)}, u32[]{:S(2)}) copy-start(f32[8,8]{1,0:T(8,128)} %param.9) | copy-start | bytes 772
  2.0 19.6 %all-to-all-start.2 = ((s32[1,32,1]{2,0,1:T(1,128)}), s32[1,32,1]{2,0,1:T(1,128)S(1)}, u32[]{:S(2)}, u32[]{:S(2)}) async-start(s32[1,32,1]{2,0,1:T(1,128)} %copy.63), calls=%async_computation.2 | async-start | bytes 32768 | tf_op jit(solution)/shard_map/all_to_all | solution.py:41
  21.6 12.2 %all-to-all-start.1 = ((s32[1,32,8]{2,0,1:T(1,128)}), s32[1,32,8]{2,0,1:T(1,128)S(1)}, u32[]{:S(2)}, u32[]{:S(2)}) async-start(s32[1,32,8]{2,0,1:T(1,128)} %copy.62), calls=%async_computation.1 | async-start | bytes 32768 | tf_op jit(solution)/shard_map/all_to_all | solution.py:40
  33.8 23.4 %all-to-all-start.3 = ((f32[1,32,8]{2,0,1:T(1,128)}), f32[1,32,8]{2,0,1:T(1,128)S(1)}, u32[]{:S(2)}, u32[]{:S(2)}) async-start(f32[1,32,8]{2,0,1:T(1,128)} %copy.64), calls=%async_computation.3 | async-start | bytes 32768 | tf_op jit(solution)/shard_map/all_to_all | solution.py:39
  57.2 25.0 %all-to-all-start = ((bf16[32,2,4096]{2,1,0:T(2,128)(2,1)}), bf16[32,2,4096]{2,1,0:T(2,128)(2,1)S(1)}, u32[]{:S(2)}, u32[]{:S(2)}) async-start(bf16[32,2,4096]{2,1,0:T(2,128)(2,1)} %reshape.158), calls=%async_computation | async-start | bytes 1048576 | tf_op jit(solution)/shard_map/all_to_all | solution.py:53
  69.1 24.1 %copy-start.7 = (s32[256,1]{0,1:T(1,128)}, s32[256,1]{0,1:T(1,128)S(1)}, u32[]{:S(2)}) copy-start(s32[256,1]{0,1:T(1,128)S(1)} %compare_select_fusion) | copy-start | bytes 3076
  102.3 7.3 %collective-permute-start.1 = (f32[32,8,1,128]{3,1,2,0:T(8,128)S(1)}, f32[32,8,1,128]{3,1,2,0:T(8,128)S(1)}, u32[]{:S(2)}, u32[]{:S(2)}) collective-permute-start(f32[32,8,1,128]{3,1,2,0:T(8,128)S(1)} %get-tuple-element.25), channel_id=1, source_target_pairs={{32,0},{64,32},{96,64},{128,96},{160,128},{192,160},{224,192},{256... | collective-permute-start | bytes 393224 | tf_op jit(solution)/shard_map/ppermute | solution.py:17
  107.6 9.3 %collective-permute-start = (f32[32,8,1,128]{3,1,2,0:T(8,128)S(1)}, f32[32,8,1,128]{3,1,2,0:T(8,128)S(1)}, u32[]{:S(2)}, u32[]{:S(2)}) collective-permute-start(f32[32,8,1,128]{3,1,2,0:T(8,128)S(1)} %get-tuple-element.24), channel_id=1, source_target_pairs={{0,32},{32,64},{64,96},{96,128},{128,160},{160,192},{192,224},{224... | collective-permute-start | bytes 393224 | tf_op jit(solution)/shard_map/ppermute | solution.py:14
  121.1 9.5 %collective-permute-start.3 = (f32[32,8,10,1]{0,1,3,2:T(8,128)S(1)}, f32[32,8,10,1]{0,1,3,2:T(8,128)}, u32[]{:S(2)}, u32[]{:S(2)}) collective-permute-start(f32[32,8,10,1]{0,1,3,2:T(8,128)S(1)} %copy.68), channel_id=1, source_target_pairs={{1,0},{2,1},{3,2},{4,3},{5,4},{6,5},{7,6},{8,7},{9,8},{10,9},{11,1... | collective-permute-start | bytes 30728 | tf_op jit(solution)/shard_map/ppermute | solution.py:17
  127.8 4.2 %collective-permute-start.2 = (f32[32,8,10,1]{0,1,3,2:T(8,128)}, f32[32,8,10,1]{0,1,3,2:T(8,128)S(1)}, u32[]{:S(2)}, u32[]{:S(2)}) collective-permute-start(f32[32,8,10,1]{0,1,3,2:T(8,128)} %copy.66), channel_id=1, source_target_pairs={{0,1},{1,2},{2,3},{3,4},{4,5},{5,6},{6,7},{7,8},{8,9},{9,10},{10,1... | collective-permute-start | bytes 30728 | tf_op jit(solution)/shard_map/ppermute | solution.py:14
  135.9 7.2 %collective-permute-start.5 = (f32[32,8,1,128]{3,1,2,0:T(8,128)S(1)}, f32[32,8,1,128]{3,1,2,0:T(8,128)S(1)}, u32[]{:S(2)}, u32[]{:S(2)}) collective-permute-start(f32[32,8,1,128]{3,1,2,0:T(8,128)S(1)} %get-tuple-element.23), channel_id=1, source_target_pairs={{32,0},{64,32},{96,64},{128,96},{160,128},{192,160},{224,192},{256... | collective-permute-start | bytes 393224 | tf_op jit(solution)/shard_map/ppermute | solution.py:17
  137.8 10.8 %collective-permute-start.4 = (f32[32,8,1,128]{3,1,2,0:T(8,128)S(1)}, f32[32,8,1,128]{3,1,2,0:T(8,128)S(1)}, u32[]{:S(2)}, u32[]{:S(2)}) collective-permute-start(f32[32,8,1,128]{3,1,2,0:T(8,128)S(1)} %get-tuple-element.22), channel_id=1, source_target_pairs={{0,32},{32,64},{64,96},{96,128},{128,160},{160,192},{192,224},{224... | collective-permute-start | bytes 393224 | tf_op jit(solution)/shard_map/ppermute | solution.py:14
  152.1 6.4 %collective-permute-start.7 = (f32[32,8,10,1]{0,1,3,2:T(8,128)S(1)}, f32[32,8,10,1]{0,1,3,2:T(8,128)S(1)}, u32[]{:S(2)}, u32[]{:S(2)}) collective-permute-start(f32[32,8,10,1]{0,1,3,2:T(8,128)S(1)} %copy.72), channel_id=1, source_target_pairs={{1,0},{2,1},{3,2},{4,3},{5,4},{6,5},{7,6},{8,7},{9,8},{10,9},{11,1... | collective-permute-start | bytes 30728 | tf_op jit(solution)/shard_map/ppermute | solution.py:17
  155.2 4.8 %collective-permute-start.6 = (f32[32,8,10,1]{0,1,3,2:T(8,128)S(1)}, f32[32,8,10,1]{0,1,3,2:T(8,128)S(1)}, u32[]{:S(2)}, u32[]{:S(2)}) collective-permute-start(f32[32,8,10,1]{0,1,3,2:T(8,128)S(1)} %copy.70), channel_id=1, source_target_pairs={{0,1},{1,2},{2,3},{3,4},{4,5},{5,6},{6,7},{7,8},{8,9},{9,10},{10,1... | collective-permute-start | bytes 30728 | tf_op jit(solution)/shard_map/ppermute | solution.py:14
  164.3 6.8 %collective-permute-start.9 = (f32[32,8,1,128]{3,1,2,0:T(8,128)S(1)}, f32[32,8,1,128]{3,1,2,0:T(8,128)S(1)}, u32[]{:S(2)}, u32[]{:S(2)}) collective-permute-start(f32[32,8,1,128]{3,1,2,0:T(8,128)S(1)} %get-tuple-element.21), channel_id=1, source_target_pairs={{32,0},{64,32},{96,64},{128,96},{160,128},{192,160},{224,192},{256... | collective-permute-start | bytes 393224 | tf_op jit(solution)/shard_map/ppermute | solution.py:17
  166.2 10.5 %collective-permute-start.8 = (f32[32,8,1,128]{3,1,2,0:T(8,128)S(1)}, f32[32,8,1,128]{3,1,2,0:T(8,128)S(1)}, u32[]{:S(2)}, u32[]{:S(2)}) collective-permute-start(f32[32,8,1,128]{3,1,2,0:T(8,128)S(1)} %get-tuple-element.20), channel_id=1, source_target_pairs={{0,32},{32,64},{64,96},{96,128},{128,160},{160,192},{192,224},{224... | collective-permute-start | bytes 393224 | tf_op jit(solution)/shard_map/ppermute | solution.py:14
  180.1 6.2 %collective-permute-start.11 = (f32[32,8,10,1]{0,1,3,2:T(8,128)S(1)}, f32[32,8,10,1]{0,1,3,2:T(8,128)S(1)}, u32[]{:S(2)}, u32[]{:S(2)}) collective-permute-start(f32[32,8,10,1]{0,1,3,2:T(8,128)S(1)} %copy.76), channel_id=1, source_target_pairs={{1,0},{2,1},{3,2},{4,3},{5,4},{6,5},{7,6},{8,7},{9,8},{10,9},{11,1... | collective-permute-start | bytes 30728 | tf_op jit(solution)/shard_map/ppermute | solution.py:17
  183.1 4.9 %collective-permute-start.10 = (f32[32,8,10,1]{0,1,3,2:T(8,128)S(1)}, f32[32,8,10,1]{0,1,3,2:T(8,128)S(1)}, u32[]{:S(2)}, u32[]{:S(2)}) collective-permute-start(f32[32,8,10,1]{0,1,3,2:T(8,128)S(1)} %copy.74), channel_id=1, source_target_pairs={{0,1},{1,2},{2,3},{3,4},{4,5},{5,6},{6,7},{7,8},{8,9},{9,10},{10,1... | collective-permute-start | bytes 30728 | tf_op jit(solution)/shard_map/ppermute | solution.py:14
  192.2 6.7 %collective-permute-start.13 = (f32[32,8,1,128]{3,1,2,0:T(8,128)S(1)}, f32[32,8,1,128]{3,1,2,0:T(8,128)S(1)}, u32[]{:S(2)}, u32[]{:S(2)}) collective-permute-start(f32[32,8,1,128]{3,1,2,0:T(8,128)S(1)} %get-tuple-element.19), channel_id=1, source_target_pairs={{32,0},{64,32},{96,64},{128,96},{160,128},{192,160},{224,192},{256... | collective-permute-start | bytes 393224 | tf_op jit(solution)/shard_map/ppermute | solution.py:17
  194.1 10.3 %collective-permute-start.12 = (f32[32,8,1,128]{3,1,2,0:T(8,128)S(1)}, f32[32,8,1,128]{3,1,2,0:T(8,128)S(1)}, u32[]{:S(2)}, u32[]{:S(2)}) collective-permute-start(f32[32,8,1,128]{3,1,2,0:T(8,128)S(1)} %get-tuple-element.18), channel_id=1, source_target_pairs={{0,32},{32,64},{64,96},{96,128},{128,160},{160,192},{192,224},{224... | collective-permute-start | bytes 393224 | tf_op jit(solution)/shard_map/ppermute | solution.py:14
  206.7 9.1 %copy-start.8 = (s32[256,1]{0,1:T(1,128)S(1)}, s32[256,1]{0,1:T(1,128)}, u32[]{:S(2)}) copy-start(s32[256,1]{0,1:T(1,128)} %copy-done.7) | copy-start | bytes 3076
  208.6 7.2 %collective-permute-start.15 = (f32[32,8,10,1]{0,1,3,2:T(8,128)S(1)}, f32[32,8,10,1]{0,1,3,2:T(8,128)}, u32[]{:S(2)}, u32[]{:S(2)}) collective-permute-start(f32[32,8,10,1]{0,1,3,2:T(8,128)S(1)} %copy.80), channel_id=1, source_target_pairs={{1,0},{2,1},{3,2},{4,3},{5,4},{6,5},{7,6},{8,7},{9,8},{10,9},{11,1... | collective-permute-start | bytes 30728 | tf_op jit(solution)/shard_map/ppermute | solution.py:17
  212.1 5.2 %collective-permute-start.14 = (f32[32,8,10,1]{0,1,3,2:T(8,128)}, f32[32,8,10,1]{0,1,3,2:T(8,128)}, u32[]{:S(2)}, u32[]{:S(2)}) collective-permute-start(f32[32,8,10,1]{0,1,3,2:T(8,128)} %copy.78), channel_id=1, source_target_pairs={{0,1},{1,2},{2,3},{3,4},{4,5},{5,6},{6,7},{7,8},{8,9},{9,10},{10,1... | collective-permute-start | bytes 30728 | tf_op jit(solution)/shard_map/ppermute | solution.py:14
  224.7 22.7 %copy-start.1 = (f32[1,8,8,128]{3,0,2,1:T(1,128)}, f32[1,8,8,128]{3,0,2,1:T(1,128)S(1)}, u32[]{:S(2)}) copy-start(f32[1,8,8,128]{3,0,2,1:T(1,128)S(1)} %fusion.32) | copy-start | bytes 98308
  (6 other events, 15.8 us)
where the time goes:
time: 249 us; the launch traced here: 247 us
  local copies, waits for them, and re-layouts  78.6 us (32%)
  starting transfers between devices  77.4 us (31%)
  waiting for transfers between devices  52.8 us (21%)
  blocking collectives  20.1 us (8%)
  other arithmetic  12.4 us (5%)
  matrix products  4.98 us (2%)
    unnamed x27, local copies, waits for them, and re-layouts  35.3 us
    ppermute x8, starting transfers between devices, padded_2(): lax.ppermute(lax.slice_in_dim(block, block.shape[dim] - width, None, axis...  25 us
    ppermute x8, waiting for transfers between devices, padded_2(): lax.ppermute(lax.slice_in_dim(block, block.shape[dim] - width, None, axis...  24 us
    ppermute x8, starting transfers between devices, padded_2(): lax.ppermute(lax.slice_in_dim(block, 0, width, axis=dim), axis, backward)  23.6 us
    all_to_all x1, blocking collectives, shards(): lax.all_to_all(read_back[:, None, :], 'tx', split_axis=0, concat_axis=1,...  20.1 us
    all_to_all x1, starting transfers between devices, shards(): lax.all_to_all(obs_count, 'tx', split_axis=1, concat_axis=0, tiled=True)  11.8 us
    all_to_all x1, waiting for transfers between devices, shards(): lax.all_to_all(ensemble, 'tx', split_axis=3, concat_axis=0, tiled=True)  11.1 us
    slice x12, local copies, waits for them, and re-layouts, padded_2(): lax.slice_in_dim(block, block.shape[dim] - width, None, axis=dim)  9.89 us
  transfers between devices with their start and end apart: 20, of which 10 were waited for; matrix products, arithmetic and copies ran while one was open for 15% of the time, Pallas kernels for 0%

commit v1 on v0

v1 whole, which is shorter than its diff:
```python
import functools

import jax
import jax.numpy as jnp
from jax import lax
from jax.experimental import pallas as pl
from jax.experimental.pallas import tpu as pltpu
from jax.sharding import PartitionSpec as P

STEPS = 4
HALO = 4
LANES = 128
GROUP = 16
CHUNKS = 2
MESH = pl.DeviceIdType.MESH
DIRS = ((-1, -1), (-1, 0), (-1, 1), (0, -1), (0, 1), (1, -1), (1, 0), (1, 1))
UP, DOWN, LEFT, RIGHT = 1, 6, 3, 4


def split3(x):
    hi = x.astype(jnp.bfloat16)
    rest = x - hi.astype(jnp.float32)
    mid = rest.astype(jnp.bfloat16)
    low = (rest - mid.astype(jnp.float32)).astype(jnp.bfloat16)
    return hi, mid, low


def diffused(own, halo, coef_own, coef_halo, keep_own, keep_halo, first, last):
    for _ in range(STEPS):
        own_down, halo_down = pltpu.roll(own, 1, 0), pltpu.roll(halo, 1, 0)
        own_up, halo_up = pltpu.roll(own, 7, 0), pltpu.roll(halo, 7, 0)
        own_sum = jnp.where(first, halo_down, own_down) + jnp.where(last, halo_up, own_up)
        halo_sum = jnp.where(first, own_down, halo_down) + jnp.where(last, own_up, halo_up)
        own_sum += pltpu.roll(own, 1, 1) + pltpu.roll(own, LANES - 1, 1)
        halo_sum += pltpu.roll(halo, 1, 1) + pltpu.roll(halo, LANES - 1, 1)
        own = keep_own * own + coef_own * own_sum
        halo = keep_halo * halo + coef_halo * halo_sum
    return own


def kernel(
    ty_num, tx_num, ens, coef, vertical, weights, pack, inc_ref, back_ref,
    tiles, edge_rows, strips, strips_in, field, strip_field, field_in, strip_field_in,
    got, out_rows, cur, cur_strip, fm, fe,
    local_sem, ens_send, ens_recv, obs_send, obs_recv, fld_send, fld_recv,
    sfl_send, sfl_recv, row_send, row_recv, str_send, str_recv, ret_send, ret_recv,
):
    f32 = jnp.float32
    levels = tiles.shape[1]
    groups = tx_num * GROUP // LANES
    per = levels // CHUNKS
    row, col = lax.axis_index("ty"), lax.axis_index("tx")

    def exists(move):
        down, right = move
        ok = None
        for shift, here, num in ((down, row, ty_num), (right, col, tx_num)):
            if shift:
                inside = here > 0 if shift < 0 else here < num - 1
                ok = inside if ok is None else jnp.logical_and(ok, inside)
        return ok

    def peer(move):
        return (row + move[0], col + move[1])

    barrier = pltpu.get_barrier_semaphore()

    @pl.loop(1, tx_num)
    def _(i):
        pl.semaphore_signal(
            barrier, inc=1, device_id=(row, lax.rem(col + i, tx_num)), device_id_type=MESH
        )

    for move in DIRS:
        if move[0]:
            @pl.when(exists(move))
            def _():
                pl.semaphore_signal(barrier, inc=1, device_id=peer(move), device_id_type=MESH)

    mine = pltpu.make_async_copy(
        ens.at[0, :, :, pl.ds(pl.multiple_of(col * LANES, LANES), LANES)],
        tiles.at[col], local_sem.at[0],
    )
    mine.start()
    mine_pack = pltpu.make_async_copy(pack.at[col], got.at[col], local_sem.at[1])
    mine_pack.start()

    lane = lax.broadcasted_iota(jnp.int32, (8, LANES), 1)
    sub = lax.broadcasted_iota(jnp.int32, (8, LANES), 0)
    low_half = lax.rem(lane, GROUP) < GROUP // 2
    upper = sub < HALO
    first, last = sub == 0, sub == 7

    def strip_of(tile):
        out = jnp.where(lane < GROUP, pltpu.roll(tile, GROUP // 2, 1), 0.0)
        for width in (16, 32, 64):
            out = out + pltpu.roll(out, width, 1)
        return out

    field[levels] = coef[...]
    strip_field[levels] = strip_of(coef[...])

    for i, move in enumerate(DIRS):
        @pl.when(jnp.logical_not(exists(move)))
        def _():
            strip_field_in[i] = jnp.zeros(strip_field_in.shape[1:], f32)
            strips_in[i] = jnp.zeros(strips_in.shape[1:], jnp.bfloat16)
        if move == DIRS[UP] or move == DIRS[DOWN]:
            @pl.when(jnp.logical_not(exists(move)))
            def _():
                field_in[int(i == DOWN)] = jnp.zeros(field_in.shape[1:], f32)
                rows = pl.ds(HALO * int(i == UP), HALO)
                edge_rows[:, :, rows] = jnp.zeros((tx_num, levels, HALO, LANES), jnp.bfloat16)

    awaited = tx_num - 1
    for move in DIRS:
        if move[0]:
            awaited = awaited + jnp.where(exists(move), 1, 0)
    pl.semaphore_wait(barrier, awaited)

    def obs_copy(to):
        return pltpu.make_async_remote_copy(
            src_ref=pack.at[to], dst_ref=got.at[col], send_sem=obs_send, recv_sem=obs_recv,
            device_id=(row, to), device_id_type=MESH,
        )

    def ens_copy(to, chunk):
        return pltpu.make_async_remote_copy(
            src_ref=ens.at[0, pl.ds(chunk * per, per), :, pl.ds(pl.multiple_of(to * LANES, LANES), LANES)],
            dst_ref=tiles.at[col, pl.ds(chunk * per, per)],
            send_sem=ens_send.at[chunk], recv_sem=ens_recv.at[chunk],
            device_id=(row, to), device_id_type=MESH,
        )

    def order(i):
        half = lax.div(i + 1, 2)
        return lax.rem(col + jnp.where(lax.rem(i, 2) == 1, half, tx_num - half), tx_num)

    @pl.loop(1, tx_num)
    def _(i):
        obs_copy(order(i)).start()

    for chunk in range(CHUNKS):
        @pl.loop(1, tx_num)
        def _(i):
            ens_copy(order(i), chunk).start()

    mine_pack.wait()
    others = pl.ds(0, tx_num - 1)
    pltpu.make_async_remote_copy(
        src_ref=pack.at[others], dst_ref=got.at[others], send_sem=obs_send, recv_sem=obs_recv,
        device_id=(row, col), device_id_type=MESH,
    ).wait_recv()
    slots = got[:, 0, :]
    wide_lane = lax.broadcasted_iota(jnp.int32, (tx_num, LANES), 1)
    level_row, column, value = [], [], []
    for j in range(8):
        cell = jnp.broadcast_to(slots[:, 8 + j : 9 + j], (tx_num, LANES)).astype(jnp.int32)
        level_row.append(jnp.where((cell >> 7) == wide_lane, 1.0, 0.0).astype(f32))
        column.append((cell & 127) == wide_lane)
        value.append(jnp.where(column[-1], jnp.broadcast_to(slots[:, j : j + 1], (tx_num, LANES)), 0.0))
    pick = jnp.concatenate(level_row, axis=0)
    spread = jnp.concatenate(split3(jnp.concatenate(value, axis=0)), axis=1)
    summed = jnp.dot(
        jnp.transpose(pick).astype(jnp.bfloat16), spread, preferred_element_type=f32
    )
    forcing = summed[:, :LANES] + summed[:, LANES : 2 * LANES] + summed[:, 2 * LANES :]
    for l in range(levels):
        tile = forcing[8 * l : 8 * l + 8]
        field[l] = tile
        strip_field[l] = strip_of(tile)

    def field_copy(i):
        side = int(i == DOWN)
        return pltpu.make_async_remote_copy(
            src_ref=field, dst_ref=field_in.at[1 - side],
            send_sem=fld_send.at[side], recv_sem=fld_recv.at[1 - side],
            device_id=peer(DIRS[i]), device_id_type=MESH,
        )

    def strip_field_copy(i):
        return pltpu.make_async_remote_copy(
            src_ref=strip_field, dst_ref=strip_field_in.at[7 - i],
            send_sem=sfl_send.at[i], recv_sem=sfl_recv.at[7 - i],
            device_id=peer(DIRS[i]), device_id_type=MESH,
        )

    def rows_copy(i, chunk):
        side = int(i == DOWN)
        cut = (slice(None), pl.ds(chunk * per, per), pl.ds(HALO * side, HALO))
        return pltpu.make_async_remote_copy(
            src_ref=tiles.at[cut], dst_ref=edge_rows.at[cut],
            send_sem=row_send.at[chunk, side], recv_sem=row_recv.at[chunk, 1 - side],
            device_id=peer(DIRS[i]), device_id_type=MESH,
        )

    def strip_copy(i, chunk):
        cut = pl.ds(chunk * per, per)
        return pltpu.make_async_remote_copy(
            src_ref=strips.at[cut], dst_ref=strips_in.at[7 - i, cut],
            send_sem=str_send.at[chunk, i], recv_sem=str_recv.at[chunk, 7 - i],
            device_id=peer(DIRS[i]), device_id_type=MESH,
        )

    for i, move in enumerate(DIRS):
        @pl.when(exists(move))
        def _():
            strip_field_copy(i).start()
            if i in (UP, DOWN):
                field_copy(i).start()

    def arrived(copy_of, i):
        copy_of(7 - i).wait_recv()

    for i, move in enumerate(DIRS):
        @pl.when(exists(move))
        def _():
            arrived(strip_field_copy, i)
            if i in (UP, DOWN):
                arrived(field_copy, i)

    def joined(here, there):
        return jnp.where(low_half, here, there)

    for l in range(levels + 1):
        fm[0, l] = field[l]
        fm[1, l] = jnp.where(upper, field_in[1, l], field_in[0, l])
        around = [strip_field_in[i, l] for i in range(8)]
        here = strip_field[l]
        fe[0, 0, l] = joined(here, around[4])
        fe[0, 1, l] = jnp.where(upper, joined(around[6], around[7]), joined(around[1], around[2]))
        fe[1, 0, l] = joined(around[3], here)
        fe[1, 1, l] = jnp.where(upper, joined(around[5], around[6]), joined(around[0], around[1]))

    mine.wait()
    for chunk in range(CHUNKS):
        cut = pl.ds(chunk * per, per)
        pltpu.make_async_remote_copy(
            src_ref=tiles.at[others, cut], dst_ref=tiles.at[others, cut],
            send_sem=ens_send.at[chunk], recv_sem=ens_recv.at[chunk],
            device_id=(row, col), device_id_type=MESH,
        ).wait_recv()
        for i in (UP, DOWN):
            @pl.when(exists(DIRS[i]))
            def _():
                rows_copy(i, chunk).start()

        @pl.loop(0, groups)
        def _(g):
            for l in range(chunk * per, (chunk + 1) * per):
                out = jnp.zeros((8, LANES), f32)
                for n in range(8):
                    tile = tiles[g * 8 + n, l].astype(f32)
                    turned = pltpu.roll(tile, (GROUP // 2 + GROUP * n) % LANES, 1)
                    out = jnp.where(lax.div(lane, GROUP) == n, turned, out)
                strips[l, g] = out.astype(jnp.bfloat16)

        for i, move in enumerate(DIRS):
            @pl.when(exists(move))
            def _():
                strip_copy(i, chunk).start()
        for i in (UP, DOWN):
            @pl.when(exists(DIRS[i]))
            def _():
                arrived(functools.partial(rows_copy, chunk=chunk), i)

        coef_own, coef_halo = fm[0, levels], fm[1, levels]
        keep_own, keep_halo = 1.0 - 4.0 * coef_own, 1.0 - 4.0 * coef_halo

        @pl.loop(0, tx_num)
        def _(k):
            for l in range(chunk * per, (chunk + 1) * per):
                own = tiles[k, l].astype(f32) * fm[0, l]
                halo = edge_rows[k, l].astype(f32) * fm[1, l]
                cur[k, l] = diffused(
                    own, halo, coef_own, coef_halo, keep_own, keep_halo, first, last
                )

        for i, move in enumerate(DIRS):
            @pl.when(exists(move))
            def _():
                arrived(functools.partial(strip_copy, chunk=chunk), i)

        @pl.loop(0, groups)
        def _(g):
            for l in range(chunk * per, (chunk + 1) * per):
                here = strips[l, g].astype(f32)
                around = [strips_in[i, l, g].astype(f32) for i in range(8)]
                sides = []
                for side in range(2):
                    if side == 0:
                        own = joined(here, around[4])
                        halo = jnp.where(
                            upper, joined(around[6], around[7]), joined(around[1], around[2])
                        )
                    else:
                        own = joined(around[3], here)
                        halo = jnp.where(
                            upper, joined(around[5], around[6]), joined(around[0], around[1])
                        )
                    c_own, c_halo = fe[side, 0, levels], fe[side, 1, levels]
                    sides.append(
                        diffused(
                            own * fe[side, 0, l], halo * fe[side, 1, l], c_own, c_halo,
                            1.0 - 4.0 * c_own, 1.0 - 4.0 * c_halo, first, last,
                        )
                    )
                cur_strip[g, l] = joined(sides[0], sides[1])

    def mixed(parts, l):
        total = None
        for m in range(max(0, l - 2), min(levels, l + 3)):
            term = vertical[l, m] * parts[m]
            total = term if total is None else total + term
        return total

    def add_member(k, sums):
        parts = [cur[k, m] for m in range(levels)]
        return tuple(
            sums[l] + (weights[k] * tiles[k, l].astype(f32)) * mixed(parts, l)
            for l in range(levels)
        )

    def add_group(g, sums):
        parts = [cur_strip[g, m] for m in range(levels)]
        scale = jnp.zeros((8, LANES), f32)
        for n in range(8):
            scale = jnp.where(lax.div(lane, GROUP) == n, weights[g * 8 + n], scale)
        return tuple(
            sums[l] + (scale * strips[l, g].astype(f32)) * mixed(parts, l) for l in range(levels)
        )

    zeros = tuple(jnp.zeros((8, LANES), f32) for _ in range(levels))
    main = lax.fori_loop(0, tx_num, add_member, zeros)
    side = lax.fori_loop(0, groups, add_group, zeros)
    increment = []
    for l in range(levels):
        edge = side[l]
        for width in (64, 32, 16):
            edge = edge + pltpu.roll(edge, width, 1)
        edge = pltpu.roll(edge, LANES - GROUP // 2, 1)
        increment.append(jnp.where((lane < HALO) | (lane >= LANES - HALO), edge, main[l]))
        inc_ref[l] = increment[-1]

    source = jnp.concatenate(increment + [jnp.zeros((LANES - 8 * levels, LANES), f32)], axis=0)
    taken = jnp.dot(
        pick.astype(jnp.bfloat16), jnp.concatenate(split3(source), axis=1),
        preferred_element_type=f32,
    )
    taken = taken[:, :LANES] + taken[:, LANES : 2 * LANES] + taken[:, 2 * LANES :]
    answer = jnp.zeros((tx_num, LANES), f32)
    for j in range(8):
        part = jnp.where(column[j], taken[tx_num * j : tx_num * (j + 1)], 0.0)
        answer = jnp.where(wide_lane == j, jnp.sum(part, axis=1, keepdims=True), answer)
    out_rows[:, 0, :] = answer

    def back_copy(to):
        return pltpu.make_async_remote_copy(
            src_ref=out_rows.at[to], dst_ref=back_ref.at[col],
            send_sem=ret_send, recv_sem=ret_recv, device_id=(row, to), device_id_type=MESH,
        )

    mine_back = pltpu.make_async_copy(out_rows.at[col], back_ref.at[col], local_sem.at[2])
    mine_back.start()

    @pl.loop(1, tx_num)
    def _(i):
        back_copy(order(i)).start()

    pltpu.make_async_remote_copy(
        src_ref=pack.at[others], dst_ref=got.at[others], send_sem=obs_send, recv_sem=obs_recv,
        device_id=(row, col), device_id_type=MESH,
    ).wait_send()
    for chunk in range(CHUNKS):
        cut = pl.ds(chunk * per, per)
        pltpu.make_async_remote_copy(
            src_ref=tiles.at[others, cut], dst_ref=tiles.at[others, cut],
            send_sem=ens_send.at[chunk], recv_sem=ens_recv.at[chunk],
            device_id=(row, col), device_id_type=MESH,
        ).wait_send()
    for i, move in enumerate(DIRS):
        @pl.when(exists(move))
        def _():
            strip_field_copy(i).wait_send()
            for chunk in range(CHUNKS):
                strip_copy(i, chunk).wait_send()
            if i in (UP, DOWN):
                field_copy(i).wait_send()
                for chunk in range(CHUNKS):
                    rows_copy(i, chunk).wait_send()
    mine_back.wait()
    pltpu.make_async_remote_copy(
        src_ref=out_rows.at[others], dst_ref=back_ref.at[others],
        send_sem=ret_send, recv_sem=ret_recv, device_id=(row, col), device_id_type=MESH,
    ).wait()


def shards(ty_num, tx_num, ensemble, diffusivity, vertical, weights, obs_value, obs_cell, obs_count):
    levels = ensemble.shape[1]
    slots = obs_value.shape[2]
    live = jnp.arange(slots, dtype=jnp.int32) < obs_count[0][:, None]
    cells = jnp.where(live, obs_cell[0], -1).astype(jnp.float32)
    pack = jnp.concatenate(
        [obs_value[0], cells, jnp.zeros((tx_num, LANES - 2 * slots), jnp.float32)], axis=1
    )[:, None, :]
    groups = tx_num * GROUP // LANES
    f32, bf16, dma = jnp.float32, jnp.bfloat16, pltpu.SemaphoreType.DMA
    vmem = pl.BlockSpec(memory_space=pltpu.VMEM)
    smem = pl.BlockSpec(memory_space=pltpu.SMEM)
    increment, back = pl.pallas_call(
        functools.partial(kernel, ty_num, tx_num),
        out_shape=(
            jax.ShapeDtypeStruct((levels, 8, LANES), f32),
            jax.ShapeDtypeStruct((tx_num, 1, LANES), f32),
        ),
        in_specs=[pl.BlockSpec(memory_space=pl.ANY), vmem, smem, smem, vmem],
        out_specs=(vmem, vmem),
        scratch_shapes=[
            pltpu.VMEM((tx_num, levels, 8, LANES), bf16),
            pltpu.VMEM((tx_num, levels, 8, LANES), bf16),
            pltpu.VMEM((levels, groups, 8, LANES), bf16),
            pltpu.VMEM((8, levels, groups, 8, LANES), bf16),
            pltpu.VMEM((levels + 1, 8, LANES), f32),
            pltpu.VMEM((levels + 1, 8, LANES), f32),
            pltpu.VMEM((2, levels + 1, 8, LANES), f32),
            pltpu.VMEM((8, levels + 1, 8, LANES), f32),
            pltpu.VMEM((tx_num, 1, LANES), f32),
            pltpu.VMEM((tx_num, 1, LANES), f32),
            pltpu.VMEM((tx_num, levels, 8, LANES), f32),
            pltpu.VMEM((groups, levels, 8, LANES), f32),
            pltpu.VMEM((2, levels + 1, 8, LANES), f32),
            pltpu.VMEM((2, 2, levels + 1, 8, LANES), f32),
            dma((3,)),
            dma((CHUNKS,)), dma((CHUNKS,)),
            dma, dma,
            dma((2,)), dma((2,)),
            dma((8,)), dma((8,)),
            dma((CHUNKS, 2)), dma((CHUNKS, 2)),
            dma((CHUNKS, 8)), dma((CHUNKS, 8)),
            dma, dma,
        ],
        compiler_params=pltpu.CompilerParams(collective_id=0, has_side_effects=True),
    )(ensemble, diffusivity, vertical, weights, pack)
    return increment, back[None, :, 0, :slots]


def solution(mesh):
    placed = (
        P("tx", None, "ty", None),
        P("ty", "tx"),
        P(),
        P(),
        P(("ty", "tx"), None, None),
        P(("ty", "tx"), None, None),
        P(("ty", "tx"), None),
    )
    return jax.shard_map(
        functools.partial(shards, mesh.shape["ty"], mesh.shape["tx"]),
        mesh=mesh,
        in_specs=placed,
        out_specs=(P(None, "ty", "tx"), P(("ty", "tx"), None, None)),
        check_vma=False,
    )
```

time: 249 us -> 78.5 us (0.32)
  starting transfers between devices: 77.4 us -> 0 us
  local copies, waits for them, and re-layouts: 78.6 us -> 4.76 us
  Pallas kernels: 0 us -> 72 us
  waiting for transfers between devices: 52.8 us -> 0 us
  blocking collectives: 20.1 us -> 0 us
  other arithmetic: 12.4 us -> 0.76 us
  matrix products: 4.98 us -> 0 us
    pallas_call x0 -> x1, Pallas kernels: none -> 72 us  [shards(): pl.pallas_call(functools.partial(kernel, ty_num, tx_num), out_shape=(jax....]
    ppermute x16 -> x0, starting transfers between devices: 48.6 us -> none  [the longest x8 25 us: padded_2(): lax.ppermute(lax.slice_in_dim(block, block.shape[dim] - width, None, axis...]
    unnamed x27 -> x10, local copies, waits for them, and re-layouts: 35.3 us -> 4.69 us
    all_to_all x4 -> x0, starting transfers between devices: 28.8 us -> none  [the longest x1 11.8 us: shards(): lax.all_to_all(obs_count, 'tx', split_axis=1, concat_axis=0, tiled=True)]
    ppermute x16 -> x0, waiting for transfers between devices: 28.7 us -> none  [the longest x8 24 us: padded_2(): lax.ppermute(lax.slice_in_dim(block, block.shape[dim] - width, None, axis...]
    all_to_all x4 -> x0, waiting for transfers between devices: 24.1 us -> none  [the longest x1 11.1 us: shards(): lax.all_to_all(ensemble, 'tx', split_axis=3, concat_axis=0, tiled=True)]
    all_to_all x1 -> x0, blocking collectives: 20.1 us -> none  [shards(): lax.all_to_all(read_back[:, None, :], 'tx', split_axis=0, concat_axis=1,...]
    slice x16 -> x0, local copies, waits for them, and re-layouts: 17.4 us -> none  [the longest x12 9.89 us: padded_2(): lax.slice_in_dim(block, block.shape[dim] - width, None, axis=dim)]
  transfers between devices with their start and end apart: 20 -> 0, of which waited for: 10 -> 0; matrix products, arithmetic and copies ran while one was open for 15% -> 0% of each run, Pallas kernels for 0% -> 0%
where the time goes in v1:
time: 78.5 us; the launch traced here: 78.1 us
  Pallas kernels  72 us (92%)
  local copies, waits for them, and re-layouts  4.76 us (6%)
    pallas_call x1, Pallas kernels, shards(): pl.pallas_call(functools.partial(kernel, ty_num, tx_num), out_shape=(jax....  72 us
    unnamed x10, local copies, waits for them, and re-layouts  4.69 us

profile of v1, /device:TPU:5, one launch (start us, length us, event | category | flops | bytes accessed | tf_op | source)
XLA Modules:
  0.0 78.1 jit_solution(15157159924549204682)
XLA Ops:
  0.6 0.0 copy-start
  0.6 0.1 pad.2.clone
  0.7 0.6 copy-done
  1.3 0.0 copy-start.1
  1.3 0.1 copy.9
  1.4 0.6 copy-done.1
  2.0 0.0 copy-start.2
  2.0 0.1 copy.10
  2.1 0.6 copy-done.2
  2.7 0.1 fusion
  2.7 0.7 maximum_maximum_fusion
  3.4 72.0 %shard_map.86 = (f32[8,8,128]{2,1,0:T(8,128)}, f32[32,1,128]{2,1,0:T(1,128)}) custom-call(bf16[1,8,8,4096]{3,2,1,0:T(8,128)(2,1)} %ens.1, f32[8,128]{1,0:T(8,128)} %coef.1, f32[8,8]{1,0:T(8,128)} %vertical.1, f32[32]{0:T(128)} %weights.1, f32[32,1,128]{2,1,0:T(1,128)} %bitcast.9), custom_call_target="tpu_custom_call" | custom-call | tf_op jit(solution)/shard_map/pallas_call | solution.py:410
  75.4 1.4 %copy.11 = f32[1,32,8]{1,2,0:T(8,128)} copy(f32[1,32,8]{2,1,0:T(8,128)} %bitcast.11) | data formatting | bytes 2048
  76.8 1.4 %copy.13 = f32[8,8,128]{2,1,0:T(8,128)} copy(f32[8,8,128]{2,1,0:T(8,128)} %get-tuple-element.10) | data formatting | bytes 65536
  (1 shorter events, 0.0 us)
Async XLA Ops:
  0.6 0.7 copy-start
  1.3 0.7 copy-start.1
  2.0 0.7 copy-start.2

commit v2 on v1

v2 whole, which is shorter than its diff:
```python
import functools

import jax
import jax.numpy as jnp
from jax import lax
from jax.experimental import pallas as pl
from jax.experimental.pallas import tpu as pltpu
from jax.sharding import PartitionSpec as P

STEPS = 4
HALO = 4
LANES = 128
GROUP = 16
CHUNKS = 2
MESH = pl.DeviceIdType.MESH
DIRS = ((-1, -1), (-1, 0), (-1, 1), (0, -1), (0, 1), (1, -1), (1, 0), (1, 1))
UP, DOWN = 1, 6
PLACE = (3, 2, 4, 0, 1, 3, 2, 4)


def split3(x):
    hi = x.astype(jnp.bfloat16)
    rest = x - hi.astype(jnp.float32)
    mid = rest.astype(jnp.bfloat16)
    low = (rest - mid.astype(jnp.float32)).astype(jnp.bfloat16)
    return hi, mid, low


def diffused(rows, coef, keep):
    width = len(rows)
    for step in range(1, STEPS + 1):
        fresh = [None] * width
        for i in range(step, width - step):
            beside = pltpu.roll(rows[i], 1, 2) + pltpu.roll(rows[i], LANES - 1, 2)
            fresh[i] = keep(i) * rows[i] + coef(i) * (beside + (rows[i - 1] + rows[i + 1]))
        rows = fresh
    return rows[STEPS : width - STEPS]


def kernel(
    ty_num, tx_num, ens, coef, vertical, weights, pack, inc_ref, back_ref,
    tiles, turned, edge_rows, strips, strips_in, field, strip_field, field_in, strip_field_in,
    got, out_rows, cur, cur_strip, spread_field, spread_strip, scale, stage, edge_sum,
    local_sem, ens_send, ens_recv, obs_send, obs_recv, fld_send, fld_recv,
    sfl_send, sfl_recv, row_send, row_recv, str_send, str_recv, ret_send, ret_recv,
):
    f32 = jnp.float32
    levels = tiles.shape[1]
    batch = min(16, tx_num)
    batches = tx_num // batch
    per = levels // CHUNKS
    row, col = lax.axis_index("ty"), lax.axis_index("tx")

    def exists(move):
        down, right = move
        ok = None
        for shift, here, num in ((down, row, ty_num), (right, col, tx_num)):
            if shift:
                inside = here > 0 if shift < 0 else here < num - 1
                ok = inside if ok is None else jnp.logical_and(ok, inside)
        return ok

    def kept_rows(i):
        return {-1: pl.ds(HALO, HALO), 0: pl.ds(0, 8), 1: pl.ds(0, HALO)}[DIRS[i][0]]

    def peer(move):
        return (row + move[0], col + move[1])

    barrier = pltpu.get_barrier_semaphore()

    @pl.loop(1, tx_num)
    def _(i):
        pl.semaphore_signal(
            barrier, inc=1, device_id=(row, lax.rem(col + i, tx_num)), device_id_type=MESH
        )

    for move in DIRS:
        if move[0]:
            @pl.when(exists(move))
            def _():
                pl.semaphore_signal(barrier, inc=1, device_id=peer(move), device_id_type=MESH)

    mine = pltpu.make_async_copy(
        ens.at[0, :, :, pl.ds(pl.multiple_of(col * LANES, LANES), LANES)],
        tiles.at[col], local_sem.at[0],
    )
    mine.start()
    mine_pack = pltpu.make_async_copy(pack.at[col], got.at[col], local_sem.at[1])
    mine_pack.start()

    lane = lax.broadcasted_iota(jnp.int32, (8, LANES), 1)
    low_half = lax.rem(lane, GROUP) < GROUP // 2

    def into_strip(strip, tile, l, lane):
        moved = pltpu.roll(tile, (GROUP // 2 + GROUP * l) % LANES, tile.ndim - 1)
        return jnp.where(lax.div(lane, GROUP) == l, moved, strip)

    def strip_of(tile):
        out = jnp.where(lane < GROUP, pltpu.roll(tile, GROUP // 2, 1), 0.0)
        for width in (16, 32, 64):
            out = out + pltpu.roll(out, width, 1)
        return out

    field[levels] = coef[...]
    strip_field[1] = strip_of(coef[...])
    for k in range(tx_num):
        scale[k : k + 1, :] = jnp.full((1, LANES), weights[k], f32)

    for i, move in enumerate(DIRS):
        @pl.when(jnp.logical_not(exists(move)))
        def _():
            rows = kept_rows(i)
            size = HALO if move[0] else 8
            strip_field_in[PLACE[i], :, rows] = jnp.zeros((2, size, LANES), f32)
            strips_in[PLACE[i], rows] = jnp.zeros((size, tx_num, LANES), jnp.bfloat16)
            if i in (UP, DOWN):
                field_in[:, rows] = jnp.zeros((levels + 1, size, LANES), f32)
                edge_rows[:, rows] = jnp.zeros((levels, size, tx_num, LANES), jnp.bfloat16)

    awaited = tx_num - 1
    for move in DIRS:
        if move[0]:
            awaited = awaited + jnp.where(exists(move), 1, 0)
    pl.semaphore_wait(barrier, awaited)

    def obs_copy(to):
        return pltpu.make_async_remote_copy(
            src_ref=pack.at[to], dst_ref=got.at[col], send_sem=obs_send, recv_sem=obs_recv,
            device_id=(row, to), device_id_type=MESH,
        )

    def ens_copy(to, chunk):
        return pltpu.make_async_remote_copy(
            src_ref=ens.at[0, pl.ds(chunk * per, per), :, pl.ds(pl.multiple_of(to * LANES, LANES), LANES)],
            dst_ref=tiles.at[col, pl.ds(chunk * per, per)],
            send_sem=ens_send.at[chunk], recv_sem=ens_recv.at[chunk],
            device_id=(row, to), device_id_type=MESH,
        )

    def order(i):
        half = lax.div(i + 1, 2)
        return lax.rem(col + jnp.where(lax.rem(i, 2) == 1, half, tx_num - half), tx_num)

    @pl.loop(1, tx_num)
    def _(i):
        obs_copy(order(i)).start()

    for chunk in range(CHUNKS):
        @pl.loop(1, tx_num)
        def _(i):
            ens_copy(order(i), chunk).start()

    mine_pack.wait()
    others = pl.ds(0, tx_num - 1)
    pltpu.make_async_remote_copy(
        src_ref=pack.at[others], dst_ref=got.at[others], send_sem=obs_send, recv_sem=obs_recv,
        device_id=(row, col), device_id_type=MESH,
    ).wait_recv()
    slots = got[:, 0, :]
    wide_lane = lax.broadcasted_iota(jnp.int32, (tx_num, LANES), 1)
    level_row, column, value = [], [], []
    for j in range(8):
        cell = jnp.broadcast_to(slots[:, 8 + j : 9 + j], (tx_num, LANES)).astype(jnp.int32)
        level_row.append(jnp.where((cell >> 7) == wide_lane, 1.0, 0.0).astype(f32))
        column.append((cell & 127) == wide_lane)
        value.append(jnp.where(column[-1], jnp.broadcast_to(slots[:, j : j + 1], (tx_num, LANES)), 0.0))
    pick = jnp.concatenate(level_row, axis=0)
    spread = jnp.concatenate(split3(jnp.concatenate(value, axis=0)), axis=1)
    summed = jnp.dot(
        jnp.transpose(pick).astype(jnp.bfloat16), spread, preferred_element_type=f32
    )
    forcing = summed[:, :LANES] + summed[:, LANES : 2 * LANES] + summed[:, 2 * LANES :]
    strip = jnp.zeros((8, LANES), f32)
    for l in range(levels):
        tile = forcing[8 * l : 8 * l + 8]
        field[l] = tile
        strip = into_strip(strip, tile, l, lane)
    strip_field[0] = strip

    def field_copy(i):
        rows = kept_rows(7 - i)
        return pltpu.make_async_remote_copy(
            src_ref=field.at[:, rows], dst_ref=field_in.at[:, rows],
            send_sem=fld_send.at[i], recv_sem=fld_recv.at[7 - i],
            device_id=peer(DIRS[i]), device_id_type=MESH,
        )

    def strip_field_copy(i):
        rows = kept_rows(7 - i)
        return pltpu.make_async_remote_copy(
            src_ref=strip_field.at[:, rows], dst_ref=strip_field_in.at[PLACE[7 - i], :, rows],
            send_sem=sfl_send.at[i], recv_sem=sfl_recv.at[7 - i],
            device_id=peer(DIRS[i]), device_id_type=MESH,
        )

    def rows_copy(i, chunk):
        cut = (pl.ds(chunk * per, per), kept_rows(7 - i))
        return pltpu.make_async_remote_copy(
            src_ref=turned.at[cut], dst_ref=edge_rows.at[cut],
            send_sem=row_send.at[chunk, i], recv_sem=row_recv.at[chunk, 7 - i],
            device_id=peer(DIRS[i]), device_id_type=MESH,
        )

    def strip_copy(i):
        rows = kept_rows(7 - i)
        return pltpu.make_async_remote_copy(
            src_ref=strips.at[rows], dst_ref=strips_in.at[PLACE[7 - i], rows],
            send_sem=str_send.at[i], recv_sem=str_recv.at[7 - i],
            device_id=peer(DIRS[i]), device_id_type=MESH,
        )

    for i, move in enumerate(DIRS):
        @pl.when(exists(move))
        def _():
            strip_field_copy(i).start()
            if i in (UP, DOWN):
                field_copy(i).start()

    def arrived(copy_of, i):
        copy_of(7 - i).wait_recv()

    def edges(here, around, half):
        def joined(one, other):
            return jnp.where(half, one, other)

        return (
            (joined(here, around[1]), joined(around[2], around[4])),
            (joined(around[0], here), joined(around[3], around[2])),
        )

    def tall(i):
        return (0, i - HALO) if HALO <= i < HALO + 8 else (1, (i + HALO) % 8)

    def spread_rows(own, halo):
        pair = (own, halo)
        out = []
        for i in range(8 + 2 * HALO):
            which, r = tall(i)
            out.append(jnp.broadcast_to(pair[which][r : r + 1], (8, LANES)))
        return out

    def finish_fields():
        for i, move in enumerate(DIRS):
            @pl.when(exists(move))
            def _():
                arrived(strip_field_copy, i)
                if i in (UP, DOWN):
                    arrived(field_copy, i)
        for l in range(levels + 1):
            for i, line in enumerate(spread_rows(field[l], field_in[l])):
                spread_field[l, i] = line
                if l == levels:
                    spread_field[levels + 1, i] = 1.0 - 4.0 * line
        for kind in range(2):
            both = edges(strip_field[kind], [strip_field_in[i, kind] for i in range(5)], low_half)
            for side in range(2):
                for i, line in enumerate(spread_rows(*both[side])):
                    spread_strip[side, kind, i] = line
                    if kind == 1:
                        spread_strip[side, 2, i] = 1.0 - 4.0 * line

    def block(value):
        return value.astype(f32).reshape(batch // 8, 8, LANES)

    def members(b):
        return pl.ds(pl.multiple_of(b * batch, batch), batch)

    def share(chunk):
        cut = pl.ds(chunk * per, per)
        pltpu.make_async_remote_copy(
            src_ref=tiles.at[others, cut], dst_ref=tiles.at[others, cut],
            send_sem=ens_send.at[chunk], recv_sem=ens_recv.at[chunk],
            device_id=(row, col), device_id_type=MESH,
        ).wait_recv()

        @pl.loop(0, batches)
        def _(b):
            for l in range(chunk * per, (chunk + 1) * per):
                slot = l % 2
                stage[slot] = tiles[members(b), l].astype(f32).reshape(batch * 8, LANES)
                for r in range(8):
                    turned[l, r, members(b)] = stage[slot, pl.ds(r, batch, stride=8)].astype(jnp.bfloat16)

        for i in (UP, DOWN):
            @pl.when(exists(DIRS[i]))
            def _():
                rows_copy(i, chunk).start()

    wide = lax.broadcasted_iota(jnp.int32, (batch // 8, 8, LANES), 2)

    def share_strips():
        @pl.loop(0, batches)
        def _(b):
            for r in range(8):
                out = jnp.zeros((batch // 8, 8, LANES), f32)
                for l in range(levels):
                    out = into_strip(out, block(turned[l, r, members(b)]), l, wide)
                strips[r, members(b)] = out.reshape(batch, LANES).astype(jnp.bfloat16)

        for i, move in enumerate(DIRS):
            @pl.when(exists(move))
            def _():
                strip_copy(i).start()

    def diffuse_main(chunk):
        for i in (UP, DOWN):
            @pl.when(exists(DIRS[i]))
            def _():
                arrived(functools.partial(rows_copy, chunk=chunk), i)

        @pl.loop(0, batches)
        def _(b):
            @pl.loop(chunk * per, (chunk + 1) * per)
            def _(l):
                rows = []
                for i in range(8 + 2 * HALO):
                    which, r = tall(i)
                    here = (turned, edge_rows)[which][l, r, members(b)]
                    rows.append(block(here) * spread_field[l, i])
                done = diffused(
                    rows, lambda i: spread_field[levels, i], lambda i: spread_field[levels + 1, i]
                )
                for r in range(8):
                    cur[l, r, members(b)] = done[r].reshape(batch, LANES)

    def diffuse_edges():
        for i, move in enumerate(DIRS):
            @pl.when(exists(move))
            def _():
                arrived(strip_copy, i)
        half = lax.rem(wide, GROUP) < GROUP // 2

        @pl.loop(0, batches)
        def _(b):
            results = []
            for side in range(2):
                rows = []
                for i in range(8 + 2 * HALO):
                    which, r = tall(i)
                    here = block(strips[r, members(b)])
                    around = [block(strips_in[n, r, members(b)]) for n in range(5)]
                    rows.append(edges(here, around, half)[side][which] * spread_strip[side, 0, i])
                results.append(
                    diffused(
                        rows, lambda i: spread_strip[side, 1, i], lambda i: spread_strip[side, 2, i]
                    )
                )
            for r in range(8):
                both = jnp.where(half, results[0][r], results[1][r])
                cur_strip[r, members(b)] = both.reshape(batch, LANES)

    mine.wait()
    share(0)
    finish_fields()
    for chunk in range(1, CHUNKS):
        share(chunk)
    share_strips()
    for chunk in range(CHUNKS):
        diffuse_main(chunk)
    diffuse_edges()

    band = []
    for shift in range(-2, 3):
        line = jnp.zeros((8, LANES), f32)
        for l in range(max(0, -shift), min(levels, levels - shift)):
            line = jnp.where(lax.div(lane, GROUP) == l, vertical[l, l + shift], line)
        band.append(line)

    def mixed(parts, l):
        total = None
        for m in range(max(0, l - 2), min(levels, l + 3)):
            term = vertical[l, m] * parts[m]
            total = term if total is None else total + term
        return total

    def folded(total):
        return jnp.sum(jnp.sum(total, axis=0), axis=0, keepdims=True)

    @pl.loop(0, 8)
    def _(r):
        sums = [jnp.zeros((batch // 8, 8, LANES), f32)] * levels
        side = jnp.zeros((batch // 8, 8, LANES), f32)
        for b in range(batches):
            some = pl.ds(b * batch, batch)
            factor = block(scale[some])
            parts = [block(cur[m, r, some]) for m in range(levels)]
            for l in range(levels):
                sums[l] = sums[l] + (factor * block(turned[l, r, some])) * mixed(parts, l)
            part = block(cur_strip[r, some])
            total = jnp.zeros((batch // 8, 8, LANES), f32)
            for shift in range(-2, 3):
                total = total + band[shift + 2] * pltpu.roll(part, (-GROUP * shift) % LANES, 2)
            side = side + (factor * block(strips[r, some])) * total
        for l in range(levels):
            inc_ref[l, pl.ds(r, 1)] = folded(sums[l])
        edge_sum[pl.ds(r, 1)] = folded(side)

    increment = []
    for l in range(levels):
        edge = pltpu.roll(edge_sum[...], (LANES - GROUP // 2 - GROUP * l) % LANES, 1)
        increment.append(jnp.where((lane < HALO) | (lane >= LANES - HALO), edge, inc_ref[l]))
        inc_ref[l] = increment[-1]

    source = jnp.concatenate(increment + [jnp.zeros((LANES - 8 * levels, LANES), f32)], axis=0)
    taken = jnp.dot(
        pick.astype(jnp.bfloat16), jnp.concatenate(split3(source), axis=1),
        preferred_element_type=f32,
    )
    taken = taken[:, :LANES] + taken[:, LANES : 2 * LANES] + taken[:, 2 * LANES :]
    answer = jnp.zeros((tx_num, LANES), f32)
    for j in range(8):
        part = jnp.where(column[j], taken[tx_num * j : tx_num * (j + 1)], 0.0)
        answer = jnp.where(wide_lane == j, jnp.sum(part, axis=1, keepdims=True), answer)
    out_rows[:, 0, :] = answer

    def back_copy(to):
        return pltpu.make_async_remote_copy(
            src_ref=out_rows.at[to], dst_ref=back_ref.at[col],
            send_sem=ret_send, recv_sem=ret_recv, device_id=(row, to), device_id_type=MESH,
        )

    mine_back = pltpu.make_async_copy(out_rows.at[col], back_ref.at[col], local_sem.at[2])
    mine_back.start()

    @pl.loop(1, tx_num)
    def _(i):
        back_copy(order(i)).start()

    pltpu.make_async_remote_copy(
        src_ref=pack.at[others], dst_ref=got.at[others], send_sem=obs_send, recv_sem=obs_recv,
        device_id=(row, col), device_id_type=MESH,
    ).wait_send()
    for chunk in range(CHUNKS):
        cut = pl.ds(chunk * per, per)
        pltpu.make_async_remote_copy(
            src_ref=tiles.at[others, cut], dst_ref=tiles.at[others, cut],
            send_sem=ens_send.at[chunk], recv_sem=ens_recv.at[chunk],
            device_id=(row, col), device_id_type=MESH,
        ).wait_send()
    for i, move in enumerate(DIRS):
        @pl.when(exists(move))
        def _():
            strip_field_copy(i).wait_send()
            strip_copy(i).wait_send()
            if i in (UP, DOWN):
                field_copy(i).wait_send()
                for chunk in range(CHUNKS):
                    rows_copy(i, chunk).wait_send()
    mine_back.wait()
    pltpu.make_async_remote_copy(
        src_ref=out_rows.at[others], dst_ref=back_ref.at[others],
        send_sem=ret_send, recv_sem=ret_recv, device_id=(row, col), device_id_type=MESH,
    ).wait()


def shards(ty_num, tx_num, ensemble, diffusivity, vertical, weights, obs_value, obs_cell, obs_count):
    levels = ensemble.shape[1]
    slots = obs_value.shape[2]
    live = jnp.arange(slots, dtype=jnp.int32) < obs_count[0][:, None]
    cells = jnp.where(live, obs_cell[0], -1).astype(jnp.float32)
    pack = jnp.concatenate(
        [obs_value[0], cells, jnp.zeros((tx_num, LANES - 2 * slots), jnp.float32)], axis=1
    )[:, None, :]
    batch = min(16, tx_num)
    f32, bf16, dma = jnp.float32, jnp.bfloat16, pltpu.SemaphoreType.DMA
    vmem = pl.BlockSpec(memory_space=pltpu.VMEM)
    smem = pl.BlockSpec(memory_space=pltpu.SMEM)
    increment, back = pl.pallas_call(
        functools.partial(kernel, ty_num, tx_num),
        out_shape=(
            jax.ShapeDtypeStruct((levels, 8, LANES), f32),
            jax.ShapeDtypeStruct((tx_num, 1, LANES), f32),
        ),
        in_specs=[pl.BlockSpec(memory_space=pl.ANY), vmem, smem, smem, vmem],
        out_specs=(vmem, vmem),
        scratch_shapes=[
            pltpu.VMEM((tx_num, levels, 8, LANES), bf16),
            pltpu.VMEM((levels, 8, tx_num, LANES), bf16),
            pltpu.VMEM((levels, 8, tx_num, LANES), bf16),
            pltpu.VMEM((8, tx_num, LANES), bf16),
            pltpu.VMEM((5, 8, tx_num, LANES), bf16),
            pltpu.VMEM((levels + 1, 8, LANES), f32),
            pltpu.VMEM((2, 8, LANES), f32),
            pltpu.VMEM((levels + 1, 8, LANES), f32),
            pltpu.VMEM((5, 2, 8, LANES), f32),
            pltpu.VMEM((tx_num, 1, LANES), f32),
            pltpu.VMEM((tx_num, 1, LANES), f32),
            pltpu.VMEM((levels, 8, tx_num, LANES), f32),
            pltpu.VMEM((8, tx_num, LANES), f32),
            pltpu.VMEM((levels + 2, 8 + 2 * HALO, 8, LANES), f32),
            pltpu.VMEM((2, 3, 8 + 2 * HALO, 8, LANES), f32),
            pltpu.VMEM((tx_num, LANES), f32),
            pltpu.VMEM((2, batch * 8, LANES), f32),
            pltpu.VMEM((8, LANES), f32),
            dma((3,)),
            dma((CHUNKS,)), dma((CHUNKS,)),
            dma, dma,
            dma((8,)), dma((8,)),
            dma((8,)), dma((8,)),
            dma((CHUNKS, 8)), dma((CHUNKS, 8)),
            dma((8,)), dma((8,)),
            dma, dma,
        ],
        compiler_params=pltpu.CompilerParams(collective_id=0, has_side_effects=True),
    )(ensemble, diffusivity, vertical, weights, pack)
    return increment, back[None, :, 0, :slots]


def solution(mesh):
    placed = (
        P("tx", None, "ty", None),
        P("ty", "tx"),
        P(),
        P(),
        P(("ty", "tx"), None, None),
        P(("ty", "tx"), None, None),
        P(("ty", "tx"), None),
    )
    return jax.shard_map(
        functools.partial(shards, mesh.shape["ty"], mesh.shape["tx"]),
        mesh=mesh,
        in_specs=placed,
        out_specs=(P(None, "ty", "tx"), P(("ty", "tx"), None, None)),
        check_vma=False,
    )
```

time: 78.5 us -> 54.9 us (0.70)
  Pallas kernels: 72 us -> 48.4 us
    pallas_call x1, Pallas kernels: 72 us -> 48.4 us  [shards(): pl.pallas_call(functools.partial(kernel, ty_num, tx_num), out_shape=(jax....]
where the time goes in v2:
time: 54.9 us; the launch traced here: 54.5 us
  Pallas kernels  48.4 us (88%)
  local copies, waits for them, and re-layouts  4.76 us (9%)
  other arithmetic  0.76 us (1%)
  between operations  0.66 us (1%)
    pallas_call x1, Pallas kernels, shards(): pl.pallas_call(functools.partial(kernel, ty_num, tx_num), out_shape=(jax....  48.4 us
    unnamed x10, local copies, waits for them, and re-layouts  4.69 us

profile of v2, /device:TPU:5, one launch (start us, length us, event | category | flops | bytes accessed | tf_op | source)
XLA Modules:
  0.0 54.5 jit_solution(4059404925577259054)
XLA Ops:
  0.6 0.0 copy-start
  0.6 0.1 pad.2.clone
  0.7 0.6 %copy-done = f32[1,32,8]{1,2,0:T(8,128)S(1)} copy-done((f32[1,32,8]{1,2,0:T(8,128)S(1)}, f32[1,32,8]{1,2,0:T(8,128)}, u32[]{:S(2)}) %copy-start) | copy-done | bytes 1048
  1.3 0.0 copy-start.1
  1.3 0.1 copy.9
  1.4 0.6 %copy-done.1 = s32[1,32,8]{1,2,0:T(8,128)S(1)} copy-done((s32[1,32,8]{1,2,0:T(8,128)S(1)}, s32[1,32,8]{1,2,0:T(8,128)}, u32[]{:S(2)}) %copy-start.1) | copy-done | bytes 1048
  2.0 0.0 copy-start.2
  2.0 0.1 copy.10
  2.1 0.6 %copy-done.2 = s32[1,32]{1,0:T(1,128)S(1)} copy-done((s32[1,32]{1,0:T(1,128)S(1)}, s32[1,32]{1,0:T(1,128)}, u32[]{:S(2)}) %copy-start.2) | copy-done | bytes 152
  2.7 0.1 fusion
  2.7 0.7 %maximum_maximum_fusion = f32[32,128]{1,0:T(8,128)} fusion(f32[32,8]{1,0:T(8,128)S(1)} %fusion, f32[32,8]{1,0:T(8,128)S(1)} %bitcast.10, f32[128]{0:T(128)S(1)} %pad.2.clone), kind=kLoop, calls=%fused_computation | loop fusion | flops 8192 | bytes 18944 | tf_op jit(solution)/shard_map/concatenate | solution.py:461
  3.4 48.4 %shard_map.86 = (f32[8,8,128]{2,1,0:T(8,128)}, f32[32,1,128]{2,1,0:T(1,128)}) custom-call(bf16[1,8,8,4096]{3,2,1,0:T(8,128)(2,1)} %ens.1, f32[8,128]{1,0:T(8,128)} %coef.1, f32[8,8]{1,0:T(8,128)} %vertical.1, f32[32]{0:T(128)} %weights.1, f32[32,1,128]{2,1,0:T(1,128)} %bitcast.9), custom_call_target="tpu_custom_call" | custom-call | tf_op jit(solution)/shard_map/pallas_call | solution.py:468
  51.8 1.4 %copy.11 = f32[1,32,8]{1,2,0:T(8,128)} copy(f32[1,32,8]{2,1,0:T(8,128)} %bitcast.11) | data formatting | bytes 2048
  53.2 1.4 %copy.13 = f32[8,8,128]{2,1,0:T(8,128)} copy(f32[8,8,128]{2,1,0:T(8,128)} %get-tuple-element.10) | data formatting | bytes 65536
  (1 shorter events, 0.0 us)
Async XLA Ops:
  0.6 0.7 %copy-start = (f32[1,32,8]{1,2,0:T(8,128)S(1)}, f32[1,32,8]{1,2,0:T(8,128)}, u32[]{:S(2)}) copy-start(f32[1,32,8]{1,2,0:T(8,128)} %param.11) | copy-start | bytes 3076
  1.3 0.7 %copy-start.1 = (s32[1,32,8]{1,2,0:T(8,128)S(1)}, s32[1,32,8]{1,2,0:T(8,128)}, u32[]{:S(2)}) copy-start(s32[1,32,8]{1,2,0:T(8,128)} %param.12) | copy-start | bytes 3076
  2.0 0.7 %copy-start.2 = (s32[1,32]{1,0:T(1,128)S(1)}, s32[1,32]{1,0:T(1,128)}, u32[]{:S(2)}) copy-start(s32[1,32]{1,0:T(1,128)} %param.13) | copy-start | bytes 388

commit v3 on v2

--- a/solution.py
+++ b/solution.py
@@ -38,7 +38,8 @@
 
 
 def kernel(
-    ty_num, tx_num, ens, coef, vertical, weights, pack, inc_ref, back_ref,
+    ty_num, tx_num, ens, coef_in, vertical_in, weights_in, value_in, cell_in, count_in, inc_ref, back_ref,
+    coef, vertical, weights, obs_value, obs_cell, obs_count, lines, pack,
     tiles, turned, edge_rows, strips, strips_in, field, strip_field, field_in, strip_field_in,
     got, out_rows, cur, cur_strip, spread_field, spread_strip, scale, stage, edge_sum,
     local_sem, ens_send, ens_recv, obs_send, obs_recv, fld_send, fld_recv,
@@ -84,9 +85,64 @@
         ens.at[0, :, :, pl.ds(pl.multiple_of(col * LANES, LANES), LANES)],
         tiles.at[col], local_sem.at[0],
     )
+    small = [
+        pltpu.make_async_copy(source, target, local_sem.at[3 + n])
+        for n, (source, target) in enumerate((
+            (value_in, obs_value), (cell_in, obs_cell), (count_in, obs_count),
+            (coef_in, coef), (vertical_in, vertical), (weights_in, weights),
+        ))
+    ]
+    for copy in small:
+        copy.start()
     mine.start()
+
+    awaited = tx_num - 1
+    for move in DIRS:
+        if move[0]:
+            awaited = awaited + jnp.where(exists(move), 1, 0)
+    pl.semaphore_wait(barrier, awaited)
+
+    def obs_copy(to):
+        return pltpu.make_async_remote_copy(
+            src_ref=pack.at[to], dst_ref=got.at[col], send_sem=obs_send, recv_sem=obs_recv,
+            device_id=(row, to), device_id_type=MESH,
+        )
+
+    def ens_copy(to, chunk):
+        return pltpu.make_async_remote_copy(
+            src_ref=ens.at[0, pl.ds(chunk * per, per), :, pl.ds(pl.multiple_of(to * LANES, LANES), LANES)],
+            dst_ref=tiles.at[col, pl.ds(chunk * per, per)],
+            send_sem=ens_send.at[chunk], recv_sem=ens_recv.at[chunk],
+            device_id=(row, to), device_id_type=MESH,
+        )
+
+    def order(i):
+        half = lax.div(i + 1, 2)
+        return lax.rem(col + jnp.where(lax.rem(i, 2) == 1, half, tx_num - half), tx_num)
+
+    def send_ens(chunk):
+        @pl.loop(1, tx_num)
+        def _(i):
+            ens_copy(order(i), chunk).start()
+
+    send_ens(0)
+
+    for copy in small:
+        copy.wait()
+    live = lax.broadcasted_iota(jnp.int32, (8, tx_num), 0) < jnp.broadcast_to(obs_count[...], (8, tx_num))
+    lines[...] = jnp.zeros(lines.shape, f32)
+    lines[0:8, 0:tx_num] = obs_value[0]
+    lines[8:16, 0:tx_num] = jnp.where(live, obs_cell[0], -1).astype(f32)
+    pack[:, 0, :] = jnp.transpose(lines[...])[0:tx_num]
     mine_pack = pltpu.make_async_copy(pack.at[col], got.at[col], local_sem.at[1])
     mine_pack.start()
+
+    @pl.loop(1, tx_num)
+    def _(i):
+        obs_copy(order(i)).start()
+
+    for chunk in range(1, CHUNKS):
+        send_ens(chunk)
 
     lane = lax.broadcasted_iota(jnp.int32, (8, LANES), 1)
     low_half = lax.rem(lane, GROUP) < GROUP // 2
@@ -116,39 +172,6 @@
             if i in (UP, DOWN):
                 field_in[:, rows] = jnp.zeros((levels + 1, size, LANES), f32)
                 edge_rows[:, rows] = jnp.zeros((levels, size, tx_num, LANES), jnp.bfloat16)
-
-    awaited = tx_num - 1
-    for move in DIRS:
-        if move[0]:
-            awaited = awaited + jnp.where(exists(move), 1, 0)
-    pl.semaphore_wait(barrier, awaited)
-
-    def obs_copy(to):
-        return pltpu.make_async_remote_copy(
-            src_ref=pack.at[to], dst_ref=got.at[col], send_sem=obs_send, recv_sem=obs_recv,
-            device_id=(row, to), device_id_type=MESH,
-        )
-
-    def ens_copy(to, chunk):
-        return pltpu.make_async_remote_copy(
-            src_ref=ens.at[0, pl.ds(chunk * per, per), :, pl.ds(pl.multiple_of(to * LANES, LANES), LANES)],
-            dst_ref=tiles.at[col, pl.ds(chunk * per, per)],
-            send_sem=ens_send.at[chunk], recv_sem=ens_recv.at[chunk],
-            device_id=(row, to), device_id_type=MESH,
-        )
-
-    def order(i):
-        half = lax.div(i + 1, 2)
-        return lax.rem(col + jnp.where(lax.rem(i, 2) == 1, half, tx_num - half), tx_num)
-
-    @pl.loop(1, tx_num)
-    def _(i):
-        obs_copy(order(i)).start()
-
-    for chunk in range(CHUNKS):
-        @pl.loop(1, tx_num)
-        def _(i):
-            ens_copy(order(i), chunk).start()
 
     mine_pack.wait()
     others = pl.ds(0, tx_num - 1)
@@ -453,27 +476,35 @@
     ).wait()
 
 
+def hand_over(slots, inc_in, back_in, inc_out, back_out):
+    inc_out[...] = inc_in[...]
+    back_out[0] = jnp.transpose(back_in[:, 0, :])[:slots]
+
+
 def shards(ty_num, tx_num, ensemble, diffusivity, vertical, weights, obs_value, obs_cell, obs_count):
     levels = ensemble.shape[1]
     slots = obs_value.shape[2]
-    live = jnp.arange(slots, dtype=jnp.int32) < obs_count[0][:, None]
-    cells = jnp.where(live, obs_cell[0], -1).astype(jnp.float32)
-    pack = jnp.concatenate(
-        [obs_value[0], cells, jnp.zeros((tx_num, LANES - 2 * slots), jnp.float32)], axis=1
-    )[:, None, :]
     batch = min(16, tx_num)
     f32, bf16, dma = jnp.float32, jnp.bfloat16, pltpu.SemaphoreType.DMA
     vmem = pl.BlockSpec(memory_space=pltpu.VMEM)
-    smem = pl.BlockSpec(memory_space=pltpu.SMEM)
+    hbm = pl.BlockSpec(memory_space=pltpu.HBM)
     increment, back = pl.pallas_call(
         functools.partial(kernel, ty_num, tx_num),
         out_shape=(
             jax.ShapeDtypeStruct((levels, 8, LANES), f32),
             jax.ShapeDtypeStruct((tx_num, 1, LANES), f32),
         ),
-        in_specs=[pl.BlockSpec(memory_space=pl.ANY), vmem, smem, smem, vmem],
+        in_specs=[hbm] * 7,
         out_specs=(vmem, vmem),
         scratch_shapes=[
+            pltpu.VMEM(diffusivity.shape, f32),
+            pltpu.SMEM(vertical.shape, f32),
+            pltpu.SMEM(weights.shape, f32),
+            pltpu.VMEM((1, slots, tx_num), f32),
+            pltpu.VMEM((1, slots, tx_num), jnp.int32),
+            pltpu.VMEM(obs_count.shape, jnp.int32),
+            pltpu.VMEM((LANES, LANES), f32),
+            pltpu.VMEM((tx_num, 1, LANES), f32),
             pltpu.VMEM((tx_num, levels, 8, LANES), bf16),
             pltpu.VMEM((levels, 8, tx_num, LANES), bf16),
             pltpu.VMEM((levels, 8, tx_num, LANES), bf16),
@@ -492,7 +523,7 @@
             pltpu.VMEM((tx_num, LANES), f32),
             pltpu.VMEM((2, batch * 8, LANES), f32),
             pltpu.VMEM((8, LANES), f32),
-            dma((3,)),
+            dma((9,)),
             dma((CHUNKS,)), dma((CHUNKS,)),
             dma, dma,
             dma((8,)), dma((8,)),
@@ -502,8 +533,20 @@
             dma, dma,
         ],
         compiler_params=pltpu.CompilerParams(collective_id=0, has_side_effects=True),
-    )(ensemble, diffusivity, vertical, weights, pack)
-    return increment, back[None, :, 0, :slots]
+    )(
+        ensemble, diffusivity, vertical, weights,
+        jnp.swapaxes(obs_value, 1, 2), jnp.swapaxes(obs_cell, 1, 2), obs_count,
+    )
+    increment, back = pl.pallas_call(
+        functools.partial(hand_over, slots),
+        out_shape=(
+            jax.ShapeDtypeStruct(increment.shape, f32),
+            jax.ShapeDtypeStruct((1, slots, tx_num), f32),
+        ),
+        in_specs=[vmem, vmem],
+        out_specs=(vmem, vmem),
+    )(increment, back)
+    return increment, jnp.swapaxes(back, 1, 2)
 
 
 def solution(mesh):

time: 54.9 us -> 51.2 us (0.933)
  local copies, waits for them, and re-layouts: 4.76 us -> 0 us
  Pallas kernels: 48.4 us -> 50.3 us
  other arithmetic: 0.76 us -> 0 us
    unnamed x10 -> x0, local copies, waits for them, and re-layouts: 4.69 us -> none
    pallas_call x0 -> x1, Pallas kernels: none -> 1.43 us  [shards(): pl.pallas_call(functools.partial(hand_over, slots), out_shape=(jax.ShapeD...]
    concatenate x1 -> x0, other arithmetic: 0.68 us -> none  [shards(): jnp.concatenate([obs_value[0], cells, jnp.zeros((tx_num, LANES - 2 * slot...]
where the time goes in v3:
time: 51.2 us; the launch traced here: 51 us
  Pallas kernels  50.3 us (98%)
  between operations  0.64 us (1%)
    pallas_call x1, Pallas kernels, shards(): pl.pallas_call(functools.partial(kernel, ty_num, tx_num), out_shape=(jax....  48.9 us
    pallas_call x1, Pallas kernels, shards(): pl.pallas_call(functools.partial(hand_over, slots), out_shape=(jax.ShapeD...  1.43 us

profile of v3, /device:TPU:5, one launch (start us, length us, event | category | flops | bytes accessed | tf_op | source)
XLA Modules:
  0.0 51.0 jit_solution(12958995569285548599)
XLA Ops:
  0.6 48.9 %shard_map.86 = (f32[8,8,128]{2,1,0:T(8,128)}, f32[32,1,128]{2,1,0:T(1,128)}) custom-call(bf16[1,8,8,4096]{3,2,1,0:T(8,128)(2,1)} %ens.1, f32[8,128]{1,0:T(8,128)} %coef_in.1, f32[8,8]{1,0:T(8,128)} %vertical_in.1, f32[32]{0:T(128)} %weights_in.1, f32[1,8,32]{2,1,0:T(8,128)} %bitcast.3, s32[1,8,32]{2,1,0:T(8,128)} %bitcast.4, s32[1,32]{1,0:T(1,128)} %count_in.1), custom_call_target="tpu_custom_call" | custom-call | tf_op jit(solution)/shard_map/pallas_call | solution.py:491
  49.5 1.4 %shard_map.87 = (f32[8,8,128]{2,1,0:T(8,128)}, f32[1,8,32]{2,1,0:T(8,128)}) custom-call(f32[8,8,128]{2,1,0:T(8,128)} %get-tuple-element.6.inc_in, f32[32,1,128]{2,1,0:T(1,128)} %get-tuple-element.7.back_in), custom_call_target="tpu_custom_call" | custom-call | tf_op jit(solution)/shard_map/pallas_call | solution.py:540

commit v4 on v3

--- a/solution.py
+++ b/solution.py
@@ -11,7 +11,7 @@
 HALO = 4
 LANES = 128
 GROUP = 16
-CHUNKS = 2
+CHUNKS = 4
 MESH = pl.DeviceIdType.MESH
 DIRS = ((-1, -1), (-1, 0), (-1, 1), (0, -1), (0, 1), (1, -1), (1, 0), (1, 1))
 UP, DOWN = 1, 6
@@ -41,7 +41,7 @@
     ty_num, tx_num, ens, coef_in, vertical_in, weights_in, value_in, cell_in, count_in, inc_ref, back_ref,
     coef, vertical, weights, obs_value, obs_cell, obs_count, lines, pack,
     tiles, turned, edge_rows, strips, strips_in, field, strip_field, field_in, strip_field_in,
-    got, out_rows, cur, cur_strip, spread_field, spread_strip, scale, stage, edge_sum,
+    got, out_rows, cur, cur_strip, spread_field, spread_strip, scale, stage, edge_sum, band,
     local_sem, ens_send, ens_recv, obs_send, obs_recv, fld_send, fld_recv,
     sfl_send, sfl_recv, row_send, row_recv, str_send, str_recv, ret_send, ret_recv,
 ):
@@ -50,6 +50,8 @@
     batch = min(16, tx_num)
     batches = tx_num // batch
     per = levels // CHUNKS
+    part = tx_num // CHUNKS
+    run = per * GROUP
     row, col = lax.axis_index("ty"), lax.axis_index("tx")
 
     def exists(move):
@@ -168,7 +170,7 @@
             rows = kept_rows(i)
             size = HALO if move[0] else 8
             strip_field_in[PLACE[i], :, rows] = jnp.zeros((2, size, LANES), f32)
-            strips_in[PLACE[i], rows] = jnp.zeros((size, tx_num, LANES), jnp.bfloat16)
+            strips_in[:, PLACE[i], rows] = jnp.zeros((CHUNKS, size, part, LANES), jnp.bfloat16)
             if i in (UP, DOWN):
                 field_in[:, rows] = jnp.zeros((levels + 1, size, LANES), f32)
                 edge_rows[:, rows] = jnp.zeros((levels, size, tx_num, LANES), jnp.bfloat16)
@@ -224,11 +226,11 @@
             device_id=peer(DIRS[i]), device_id_type=MESH,
         )
 
-    def strip_copy(i):
+    def strip_copy(i, chunk):
         rows = kept_rows(7 - i)
         return pltpu.make_async_remote_copy(
-            src_ref=strips.at[rows], dst_ref=strips_in.at[PLACE[7 - i], rows],
-            send_sem=str_send.at[i], recv_sem=str_recv.at[7 - i],
+            src_ref=strips.at[chunk, rows], dst_ref=strips_in.at[chunk, PLACE[7 - i], rows],
+            send_sem=str_send.at[chunk, i], recv_sem=str_recv.at[chunk, 7 - i],
             device_id=peer(DIRS[i]), device_id_type=MESH,
         )
 
@@ -274,16 +276,31 @@
                 spread_field[l, i] = line
                 if l == levels:
                     spread_field[levels + 1, i] = 1.0 - 4.0 * line
-        for kind in range(2):
-            both = edges(strip_field[kind], [strip_field_in[i, kind] for i in range(5)], low_half)
+
+        def repeated(strip, chunk):
+            out = jnp.where(lane < run, pltpu.roll(strip, (-run * chunk) % LANES, 1), 0.0)
+            width = run
+            while width < LANES:
+                out = out + pltpu.roll(out, width, 1)
+                width *= 2
+            return out
+
+        for chunk in range(CHUNKS):
+            both = edges(
+                repeated(strip_field[0], chunk),
+                [repeated(strip_field_in[i, 0], chunk) for i in range(5)], low_half,
+            )
             for side in range(2):
                 for i, line in enumerate(spread_rows(*both[side])):
-                    spread_strip[side, kind, i] = line
-                    if kind == 1:
-                        spread_strip[side, 2, i] = 1.0 - 4.0 * line
+                    spread_strip[side, 2 + chunk, i] = line
+        both = edges(strip_field[1], [strip_field_in[i, 1] for i in range(5)], low_half)
+        for side in range(2):
+            for i, line in enumerate(spread_rows(*both[side])):
+                spread_strip[side, 0, i] = line
+                spread_strip[side, 1, i] = 1.0 - 4.0 * line
 
     def block(value):
-        return value.astype(f32).reshape(batch // 8, 8, LANES)
+        return value.astype(f32).reshape(value.shape[0] // 8, 8, LANES)
 
     def members(b):
         return pl.ds(pl.multiple_of(b * batch, batch), batch)
@@ -309,21 +326,22 @@
             def _():
                 rows_copy(i, chunk).start()
 
-    wide = lax.broadcasted_iota(jnp.int32, (batch // 8, 8, LANES), 2)
-
-    def share_strips():
-        @pl.loop(0, batches)
-        def _(b):
-            for r in range(8):
-                out = jnp.zeros((batch // 8, 8, LANES), f32)
-                for l in range(levels):
-                    out = into_strip(out, block(turned[l, r, members(b)]), l, wide)
-                strips[r, members(b)] = out.reshape(batch, LANES).astype(jnp.bfloat16)
+    wide = lax.broadcasted_iota(jnp.int32, (part // 8, 8, LANES), 2)
+
+    def share_strips(chunk):
+        @pl.loop(0, 8)
+        def _(r):
+            out = jnp.zeros((part // 8, 8, LANES), f32)
+            for n in range(CHUNKS):
+                for l in range(per):
+                    here = turned[chunk * per + l, r, pl.ds(n * part, part)]
+                    out = into_strip(out, block(here), n * per + l, wide)
+            strips[chunk, r] = out.reshape(part, LANES).astype(jnp.bfloat16)
 
         for i, move in enumerate(DIRS):
             @pl.when(exists(move))
             def _():
-                strip_copy(i).start()
+                strip_copy(i, chunk).start()
 
     def diffuse_main(chunk):
         for i in (UP, DOWN):
@@ -346,48 +364,59 @@
                 for r in range(8):
                     cur[l, r, members(b)] = done[r].reshape(batch, LANES)
 
-    def diffuse_edges():
+    def diffuse_edges(chunk):
         for i, move in enumerate(DIRS):
             @pl.when(exists(move))
             def _():
-                arrived(strip_copy, i)
+                arrived(functools.partial(strip_copy, chunk=chunk), i)
         half = lax.rem(wide, GROUP) < GROUP // 2
-
-        @pl.loop(0, batches)
-        def _(b):
-            results = []
-            for side in range(2):
-                rows = []
-                for i in range(8 + 2 * HALO):
-                    which, r = tall(i)
-                    here = block(strips[r, members(b)])
-                    around = [block(strips_in[n, r, members(b)]) for n in range(5)]
-                    rows.append(edges(here, around, half)[side][which] * spread_strip[side, 0, i])
-                results.append(
-                    diffused(
-                        rows, lambda i: spread_strip[side, 1, i], lambda i: spread_strip[side, 2, i]
-                    )
-                )
-            for r in range(8):
-                both = jnp.where(half, results[0][r], results[1][r])
-                cur_strip[r, members(b)] = both.reshape(batch, LANES)
+        results = []
+        for side in range(2):
+            rows = []
+            for i in range(8 + 2 * HALO):
+                which, r = tall(i)
+                here = block(strips[chunk, r])
+                around = [block(strips_in[chunk, n, r]) for n in range(5)]
+                rows.append(edges(here, around, half)[side][which] * spread_strip[side, 2 + chunk, i])
+            results.append(
+                diffused(rows, lambda i: spread_strip[side, 0, i], lambda i: spread_strip[side, 1, i])
+            )
+        for r in range(8):
+            both = jnp.where(half, results[0][r], results[1][r])
+            cur_strip[chunk, r] = both.reshape(part, LANES)
 
     mine.wait()
     share(0)
+    share_strips(0)
     finish_fields()
     for chunk in range(1, CHUNKS):
+        if chunk == CHUNKS - 1:
+            for early in range(CHUNKS - 3):
+                diffuse_main(early)
+                diffuse_edges(early)
         share(chunk)
-    share_strips()
+        share_strips(chunk)
+    for chunk in range(CHUNKS - 3, CHUNKS):
+        diffuse_main(chunk)
+        diffuse_edges(chunk)
+
+    bands = []
+    strip_level = lax.rem(lax.div(lane, GROUP), per)
     for chunk in range(CHUNKS):
-        diffuse_main(chunk)
-    diffuse_edges()
-
-    band = []
-    for shift in range(-2, 3):
-        line = jnp.zeros((8, LANES), f32)
-        for l in range(max(0, -shift), min(levels, levels - shift)):
-            line = jnp.where(lax.div(lane, GROUP) == l, vertical[l, l + shift], line)
-        band.append(line)
+        for other in range(CHUNKS):
+            for shift in range(1 - per, per):
+                line = None
+                for l in range(max(0, -shift), min(per, per - shift)):
+                    target, source = chunk * per + l, other * per + l + shift
+                    if abs(target - source) <= 2:
+                        line = jnp.zeros((8, LANES), f32) if line is None else line
+                        line = jnp.where(strip_level == l, vertical[target, source], line)
+                if line is not None:
+                    bands.append((chunk, other, shift))
+                    band[len(bands) - 1] = line
+    strip_scale = block(scale[pl.ds(0, part)])
+    for n in range(1, CHUNKS):
+        strip_scale = jnp.where(lax.div(wide, run) == n, block(scale[pl.ds(n * part, part)]), strip_scale)
 
     def mixed(parts, l):
         total = None
@@ -402,25 +431,36 @@
     @pl.loop(0, 8)
     def _(r):
         sums = [jnp.zeros((batch // 8, 8, LANES), f32)] * levels
-        side = jnp.zeros((batch // 8, 8, LANES), f32)
         for b in range(batches):
             some = pl.ds(b * batch, batch)
             factor = block(scale[some])
             parts = [block(cur[m, r, some]) for m in range(levels)]
             for l in range(levels):
                 sums[l] = sums[l] + (factor * block(turned[l, r, some])) * mixed(parts, l)
-            part = block(cur_strip[r, some])
-            total = jnp.zeros((batch // 8, 8, LANES), f32)
-            for shift in range(-2, 3):
-                total = total + band[shift + 2] * pltpu.roll(part, (-GROUP * shift) % LANES, 2)
-            side = side + (factor * block(strips[r, some])) * total
         for l in range(levels):
             inc_ref[l, pl.ds(r, 1)] = folded(sums[l])
-        edge_sum[pl.ds(r, 1)] = folded(side)
+        lines_of = [block(cur_strip[n, r]) for n in range(CHUNKS)]
+        totals = [jnp.zeros((part // 8, 8, LANES), f32)] * CHUNKS
+        for n, (chunk, other, shift) in enumerate(bands):
+            moved = lines_of[other]
+            if shift:
+                moved = pltpu.roll(moved, (-GROUP * shift) % LANES, 2)
+            totals[chunk] = totals[chunk] + band[n] * moved
+        for chunk in range(CHUNKS):
+            weighted = (strip_scale * block(strips[chunk, r])) * totals[chunk]
+            edge_sum[chunk, pl.ds(r, 1)] = folded(weighted)
+
+    edge_sums = []
+    for chunk in range(CHUNKS):
+        edge, width = edge_sum[chunk], LANES // 2
+        while width >= run:
+            edge = edge + pltpu.roll(edge, width, 1)
+            width //= 2
+        edge_sums.append(edge)
 
     increment = []
     for l in range(levels):
-        edge = pltpu.roll(edge_sum[...], (LANES - GROUP // 2 - GROUP * l) % LANES, 1)
+        edge = pltpu.roll(edge_sums[l // per], (LANES - GROUP // 2 - GROUP * (l % per)) % LANES, 1)
         increment.append(jnp.where((lane < HALO) | (lane >= LANES - HALO), edge, inc_ref[l]))
         inc_ref[l] = increment[-1]
 
@@ -464,7 +504,8 @@
         @pl.when(exists(move))
         def _():
             strip_field_copy(i).wait_send()
-            strip_copy(i).wait_send()
+            for chunk in range(CHUNKS):
+                strip_copy(i, chunk).wait_send()
             if i in (UP, DOWN):
                 field_copy(i).wait_send()
                 for chunk in range(CHUNKS):
@@ -484,7 +525,7 @@
 def shards(ty_num, tx_num, ensemble, diffusivity, vertical, weights, obs_value, obs_cell, obs_count):
     levels = ensemble.shape[1]
     slots = obs_value.shape[2]
-    batch = min(16, tx_num)
+    batch, part = min(16, tx_num), tx_num // CHUNKS
     f32, bf16, dma = jnp.float32, jnp.bfloat16, pltpu.SemaphoreType.DMA
     vmem = pl.BlockSpec(memory_space=pltpu.VMEM)
     hbm = pl.BlockSpec(memory_space=pltpu.HBM)
@@ -508,8 +549,8 @@
             pltpu.VMEM((tx_num, levels, 8, LANES), bf16),
             pltpu.VMEM((levels, 8, tx_num, LANES), bf16),
             pltpu.VMEM((levels, 8, tx_num, LANES), bf16),
-            pltpu.VMEM((8, tx_num, LANES), bf16),
-            pltpu.VMEM((5, 8, tx_num, LANES), bf16),
+            pltpu.VMEM((CHUNKS, 8, part, LANES), bf16),
+            pltpu.VMEM((CHUNKS, 5, 8, part, LANES), bf16),
             pltpu.VMEM((levels + 1, 8, LANES), f32),
             pltpu.VMEM((2, 8, LANES), f32),
             pltpu.VMEM((levels + 1, 8, LANES), f32),
@@ -517,19 +558,20 @@
             pltpu.VMEM((tx_num, 1, LANES), f32),
             pltpu.VMEM((tx_num, 1, LANES), f32),
             pltpu.VMEM((levels, 8, tx_num, LANES), f32),
-            pltpu.VMEM((8, tx_num, LANES), f32),
+            pltpu.VMEM((CHUNKS, 8, part, LANES), f32),
             pltpu.VMEM((levels + 2, 8 + 2 * HALO, 8, LANES), f32),
-            pltpu.VMEM((2, 3, 8 + 2 * HALO, 8, LANES), f32),
+            pltpu.VMEM((2, 2 + CHUNKS, 8 + 2 * HALO, 8, LANES), f32),
             pltpu.VMEM((tx_num, LANES), f32),
             pltpu.VMEM((2, batch * 8, LANES), f32),
-            pltpu.VMEM((8, LANES), f32),
+            pltpu.VMEM((CHUNKS, 8, LANES), f32),
+            pltpu.VMEM((64, 8, LANES), f32),
             dma((9,)),
             dma((CHUNKS,)), dma((CHUNKS,)),
             dma, dma,
             dma((8,)), dma((8,)),
             dma((8,)), dma((8,)),
             dma((CHUNKS, 8)), dma((CHUNKS, 8)),
-            dma((8,)), dma((8,)),
+            dma((CHUNKS, 8)), dma((CHUNKS, 8)),
             dma, dma,
         ],
         compiler_params=pltpu.CompilerParams(collective_id=0, has_side_effects=True),

time: 51.2 us -> 49.7 us (0.971)
  Pallas kernels: 50.3 us -> 48.9 us
    pallas_call x1, Pallas kernels: 48.9 us -> 47.4 us  [shards(): pl.pallas_call(functools.partial(kernel, ty_num, tx_num), out_shape=(jax....]
where the time goes in v4:
time: 49.7 us; the launch traced here: 49.5 us
  Pallas kernels  48.9 us (98%)
  between operations  0.64 us (1%)
    pallas_call x1, Pallas kernels, shards(): pl.pallas_call(functools.partial(kernel, ty_num, tx_num), out_shape=(jax....  47.4 us
    pallas_call x1, Pallas kernels, shards(): pl.pallas_call(functools.partial(hand_over, slots), out_shape=(jax.ShapeD...  1.43 us

profile of v4, /device:TPU:5, one launch (start us, length us, event | category | flops | bytes accessed | tf_op | source)
XLA Modules:
  0.0 49.5 jit_solution(17568977155051957675)
XLA Ops:
  0.6 47.4 %shard_map.86 = (f32[8,8,128]{2,1,0:T(8,128)}, f32[32,1,128]{2,1,0:T(1,128)}) custom-call(bf16[1,8,8,4096]{3,2,1,0:T(8,128)(2,1)} %ens.1, f32[8,128]{1,0:T(8,128)} %coef_in.1, f32[8,8]{1,0:T(8,128)} %vertical_in.1, f32[32]{0:T(128)} %weights_in.1, f32[1,8,32]{2,1,0:T(8,128)} %bitcast.3, s32[1,8,32]{2,1,0:T(8,128)} %bitcast.4, s32[1,32]{1,0:T(1,128)} %count_in.1), custom_call_target="tpu_custom_call" | custom-call | tf_op jit(solution)/shard_map/pallas_call | solution.py:532
  48.1 1.4 %shard_map.87 = (f32[8,8,128]{2,1,0:T(8,128)}, f32[1,8,32]{2,1,0:T(8,128)}) custom-call(f32[8,8,128]{2,1,0:T(8,128)} %get-tuple-element.6.inc_in, f32[32,1,128]{2,1,0:T(1,128)} %get-tuple-element.7.back_in), custom_call_target="tpu_custom_call" | custom-call | tf_op jit(solution)/shard_map/pallas_call | solution.py:582

commit v5 on v4

--- a/solution.py
+++ b/solution.py
@@ -119,11 +119,12 @@
         )
 
     def order(i):
-        half = lax.div(i + 1, 2)
-        return lax.rem(col + jnp.where(lax.rem(i, 2) == 1, half, tx_num - half), tx_num)
+        centre, away = tx_num // 4 + tx_num // 2 * lax.rem(i, 2), lax.div(i + 2, 4)
+        side = jnp.where(lax.rem(lax.div(i, 2), 2) == 1, away, tx_num - away)
+        return lax.rem(col + centre + side, tx_num)
 
     def send_ens(chunk):
-        @pl.loop(1, tx_num)
+        @pl.loop(0, tx_num - 1)
         def _(i):
             ens_copy(order(i), chunk).start()
 
@@ -139,7 +140,7 @@
     mine_pack = pltpu.make_async_copy(pack.at[col], got.at[col], local_sem.at[1])
     mine_pack.start()
 
-    @pl.loop(1, tx_num)
+    @pl.loop(0, tx_num - 1)
     def _(i):
         obs_copy(order(i)).start()
 
@@ -351,8 +352,7 @@
 
         @pl.loop(0, batches)
         def _(b):
-            @pl.loop(chunk * per, (chunk + 1) * per)
-            def _(l):
+            for l in range(chunk * per, (chunk + 1) * per):
                 rows = []
                 for i in range(8 + 2 * HALO):
                     which, r = tall(i)
@@ -485,7 +485,7 @@
     mine_back = pltpu.make_async_copy(out_rows.at[col], back_ref.at[col], local_sem.at[2])
     mine_back.start()
 
-    @pl.loop(1, tx_num)
+    @pl.loop(0, tx_num - 1)
     def _(i):
         back_copy(order(i)).start()
 

time: 49.7 us -> 49.1 us (0.988)
  Pallas kernels: 48.9 us -> 48.3 us
    pallas_call x1, Pallas kernels: 47.4 us -> 46.8 us  [shards(): pl.pallas_call(functools.partial(kernel, ty_num, tx_num), out_shape=(jax....]
where the time goes in v5:
time: 49.1 us; the launch traced here: 48.9 us
  Pallas kernels  48.3 us (98%)
  between operations  0.64 us (1%)
    pallas_call x1, Pallas kernels, shards(): pl.pallas_call(functools.partial(kernel, ty_num, tx_num), out_shape=(jax....  46.8 us
    pallas_call x1, Pallas kernels, shards(): pl.pallas_call(functools.partial(hand_over, slots), out_shape=(jax.ShapeD...  1.43 us

profile of v5, /device:TPU:5, one launch (start us, length us, event | category | flops | bytes accessed | tf_op | source)
XLA Modules:
  0.0 48.9 jit_solution(14475452987052202615)
XLA Ops:
  0.6 46.8 %shard_map.86 = (f32[8,8,128]{2,1,0:T(8,128)}, f32[32,1,128]{2,1,0:T(1,128)}) custom-call(bf16[1,8,8,4096]{3,2,1,0:T(8,128)(2,1)} %ens.1, f32[8,128]{1,0:T(8,128)} %coef_in.1, f32[8,8]{1,0:T(8,128)} %vertical_in.1, f32[32]{0:T(128)} %weights_in.1, f32[1,8,32]{2,1,0:T(8,128)} %bitcast.3, s32[1,8,32]{2,1,0:T(8,128)} %bitcast.4, s32[1,32]{1,0:T(1,128)} %count_in.1), custom_call_target="tpu_custom_call" | custom-call | tf_op jit(solution)/shard_map/pallas_call | solution.py:532
  47.5 1.4 %shard_map.87 = (f32[8,8,128]{2,1,0:T(8,128)}, f32[1,8,32]{2,1,0:T(8,128)}) custom-call(f32[8,8,128]{2,1,0:T(8,128)} %get-tuple-element.6.inc_in, f32[32,1,128]{2,1,0:T(1,128)} %get-tuple-element.7.back_in), custom_call_target="tpu_custom_call" | custom-call | tf_op jit(solution)/shard_map/pallas_call | solution.py:582
